TPU v7x, 256 devices: a whole 4x4x8 slice. The times are simulated.
256 devices in a mesh: dp: 16 (over z_hi, y, core), expert: 16 (over x, z_lo).
Axes of the slice: x: 4, y: 4, z: 8 (z_hi: 2, z_lo: 4; z = z_hi * 4 + z_lo), core: 2. Of those that a mesh axis runs over, the one named last changes fastest.
Arguments:
- images: bfloat16 [1024, 256, 1280], P(('dp', 'expert')), may hold values from -16 to 16
- router: bfloat16 [1280, 128], replicated, as said below
- w_in: bfloat16 [256, 1280, 1280], P(('dp', 'expert')), may hold values from -0.15625 to 0.15625
- w_out: bfloat16 [256, 1280, 1280], P(('dp', 'expert')), may hold values from -0.125 to 0.125
- keep_bits: int32 [1024, 256, 128], P(None, ('dp', 'expert')), may hold values from 0 to 1023, as said below
Outputs:
- mixed: bfloat16 [1024, 256, 1280], P(('dp', 'expert'))
Inputs may be any that keep to these rules, and one draw needn't show every extreme that they name: `router`: each entry within 18 / sqrt(1280) in magnitude. `keep_bits`: bit i of word w stands for hidden unit 10 * w + i.
All inputs are finite; a program needn't handle non-finite values.
Results may differ from a plain program's by a relative error of at most 0.017.
Values may be sent and summed in bfloat16 or wider, within the bound.
A program may use at most 128 MiB of HBM per device.

v0:
```python
import jax
import jax.numpy as jnp
from jax import lax
from jax.sharding import PartitionSpec as P

SPLIT = 2


keep_rate = 0.875


def unpack_flags(words):
    shifts = jnp.arange(10, dtype=jnp.int32)
    flags = jnp.right_shift(words[..., None], shifts) & 1
    return flags.reshape(words.shape[:-1] + (words.shape[-1] * 10,)).astype(jnp.float32)


def expert_piece(slot_rows, w_in, w_out, kept_units):
    pre_act = jnp.dot(slot_rows, w_in[0], preferred_element_type=jnp.float32)
    hidden = (jax.nn.gelu(pre_act) * kept_units * (1.0 / keep_rate)).astype(jnp.bfloat16)
    return jnp.dot(hidden, w_out[0], preferred_element_type=jnp.float32).astype(jnp.bfloat16)


def on_device(images, router, w_in, w_out, keep_bits):
    image_count = images.shape[0]
    width = images.shape[2]
    experts = router.shape[1]
    dp_count = lax.axis_size("dp")
    expert_count = lax.axis_size("expert")
    logits = jnp.einsum("bmd,de->bme", images, router, preferred_element_type=jnp.float32)
    dispatch = jax.nn.softmax(logits, axis=1).astype(jnp.bfloat16)
    combine = jax.nn.softmax(logits, axis=2).astype(jnp.bfloat16)
    slot_values = jnp.einsum(
        "bme,bmd->bed", dispatch, images, preferred_element_type=jnp.float32
    ).astype(jnp.bfloat16)
    kept_units = unpack_flags(keep_bits[:, 0, :])
    doubled = jnp.repeat(slot_values, SPLIT, axis=1).reshape(
        image_count, dp_count, expert_count, width
    )
    across = lax.all_to_all(doubled, "expert", split_axis=2, concat_axis=0, tiled=True)
    arrived = lax.all_to_all(across, "dp", split_axis=1, concat_axis=0, tiled=True)
    partial_value = expert_piece(arrived.reshape(-1, width), w_in, w_out, kept_units)
    returned = lax.all_to_all(
        partial_value.reshape(-1, 1, 1, width), "dp", split_axis=0, concat_axis=1, tiled=True
    )
    returned = lax.all_to_all(returned, "expert", split_axis=0, concat_axis=2, tiled=True)
    paired = returned.reshape(image_count, experts, SPLIT, width)
    expert_out = paired.astype(jnp.float32).sum(axis=2).astype(jnp.bfloat16)
    mixed = jnp.einsum("bme,bed->bmd", combine, expert_out, preferred_element_type=jnp.float32)
    return mixed.astype(jnp.bfloat16)


def solution(mesh):
    placed = (
        P(("dp", "expert"), None, None),
        P(),
        P(("dp", "expert"), None, None),
        P(("dp", "expert"), None, None),
        P(None, ("dp", "expert"), None),
    )
    return jax.shard_map(
        on_device,
        mesh=mesh,
        in_specs=placed,
        out_specs=P(("dp", "expert"), None, None),
        check_vma=False,
    )
```

profile of v0, /device:TPU:1, one launch (start us, length us, event | category | flops | bytes accessed | tf_op | source)
XLA Modules:
  0.0 342.5 jit_solution(12739725940960338433)
XLA Ops:
  0.0 2.7 fusion.27
  2.8 0.8 copy-done.2
  3.6 0.1 fusion.39
  3.7 3.7 %convolution_convert_fusion.2 = bf16[4,128,1280]{2,1,0:T(8,128)(2,1)} fusion(bf16[4,256,1280]{2,1,0:T(8,128)(2,1)} %param.5, f32[4,128]{1,0:T(4,128)S(1)} %fusion.39, f32[4,256,128]{2,1,0:T(8,128)} %copy-done.2), kind=kOutput, calls=%fused_computation.19 | convolution fusion | flops 336593664 | bytes 4458496 | tf_op jit(solution)/shard_map/bme,bmd->bed/dot_general | solution.py:33
  7.4 2.3 copy.31
  9.8 0.7 broadcast_in_dim.2
  10.5 1.2 copy.32
  11.7 69.5 %all_to_all.66 = bf16[4,16,16,1280]{3,0,1,2:T(4,128)(2,1)S(1)} all-to-all(bf16[4,16,16,1280]{3,0,1,2:T(4,128)(2,1)S(1)} %copy.32), channel_id=1, replica_groups=mesh['dp'=16,'expert'=16] {'expert'}, dimensions={2} | all-to-all | bytes 5242880 | tf_op jit(solution)/shard_map/all_to_all | solution.py:40
  81.2 0.4 copy.33
  81.6 2.3 copy.34
  83.9 10.1 %all-to-all-start.1 = ((bf16[64,16,1,1280]{3,0,2,1:T(8,128)(2,1)}), bf16[64,16,1,1280]{3,0,2,1:T(8,128)(2,1)}, u32[]{:S(2)}, u32[]{:S(2)}) async-start(bf16[64,16,1,1280]{3,0,2,1:T(8,128)(2,1)} %copy.34), calls=%async_computation.1 | async-start | bytes 5242880 | tf_op jit(solution)/shard_map/all_to_all | solution.py:41
  94.0 2.1 copy.37
  96.1 5.4 %shift_right_arithmetic.23 = s32[1024,128,10]{0,2,1:T(8,128)} broadcast(s32[1024,128]{0,1:T(8,128)} %copy.37), dimensions={0,1} | broadcast | bytes 5767168 | tf_op jit(solution)/shard_map/shift_right_arithmetic | solution.py:14
  101.5 7.9 %shift_right_arithmetic.24 = s32[1024,1280]{0,1:T(8,128)} reshape(s32[1024,128,10]{0,2,1:T(8,128)} %shift_right_arithmetic.23) | data formatting | bytes 10485760 | tf_op jit(solution)/shard_map/shift_right_arithmetic | solution.py:14
  109.4 5.9 %copy.38 = s32[1024,1280]{1,0:T(8,128)} copy(s32[1024,1280]{0,1:T(8,128)} %shift_right_arithmetic.24) | data formatting | bytes 10485760 | tf_op jit(solution)/shard_map/shift_right_arithmetic | solution.py:14
  115.5 41.3 %all-to-all-done.1 = bf16[64,16,1,1280]{3,0,2,1:T(8,128)(2,1)} async-done(((bf16[64,16,1,1280]{3,0,2,1:T(8,128)(2,1)}), bf16[64,16,1,1280]{3,0,2,1:T(8,128)(2,1)}, u32[]{:S(2)}, u32[]{:S(2)}) %all-to-all-start.1) | async-done | bytes 2621472 | tf_op jit(solution)/shard_map/all_to_all | solution.py:41
  156.8 3.2 copy.48
  159.9 2.3 copy.36
  162.2 11.8 %fusion.17 = bf16[1024,1,1,1280]{3,0,2,1:T(8,128)(2,1)} fusion(bf16[1,1280,1280]{2,1,0:T(8,128)(2,1)S(1)} %copy-done, s32[1024,1280]{1,0:T(8,128)} %copy.38, bf16[1024,1280]{1,0:T(8,128)(2,1)} %bitcast.54, bf16[1,1280,1280]{2,1,0:T(8,128)(2,1)} %param.7, s32[1280]{0:T(1024)S(1)} %shift_right_arithmetic.26), kind=kOutput, calls=%fused_computation.18 | convolution fusion | flops 6730547200 | bytes 17044480 | tf_op jit(solution)/shard_map/dot_general | solution.py:21
  174.0 0.5 broadcast.8
  174.6 4.5 %reduce.1 = bf16[1024,1280]{1,0:T(8,128)(2,1)S(1)} reduce(bf16[1024,1,1,1280]{3,0,2,1:T(8,128)(2,1)} %fusion.17, bf16[]{:T(256)} %broadcast.8), dimensions={1,2}, to_apply=%copy.39.reduce_sub_computation | reduce | bytes 5242882 | tf_op jit(solution)/shard_map/reshape | solution.py:44
  179.0 2.2 reshape.23
  181.2 57.8 %all_to_all.67 = bf16[16,2,40960]{2,1,0:T(2,128)(2,1)S(1)} all-to-all(bf16[16,2,40960]{2,1,0:T(2,128)(2,1)} %reshape.23), channel_id=1, replica_groups=mesh['dp'=16,'expert'=16] {'dp'}, dimensions={0} | all-to-all | bytes 5242880 | tf_op jit(solution)/shard_map/all_to_all | solution.py:43
  239.0 7.2 %reshape.24 = bf16[1024,1,1,1280]{3,2,1,0:T(2,128)(2,1)} reshape(bf16[16,2,40960]{2,1,0:T(2,128)(2,1)S(1)} %all_to_all.67) | data formatting | bytes 5242880
  246.2 2.9 copy.44
  249.1 2.9 copy.40
  252.0 15.0 %all-to-all-start.3 = ((bf16[64,16,1,1280]{3,1,2,0:T(8,128)(2,1)}), bf16[64,16,1,1280]{3,1,2,0:T(8,128)(2,1)S(1)}, u32[]{:S(2)}, u32[]{:S(2)}) async-start(bf16[64,16,1,1280]{3,1,2,0:T(8,128)(2,1)} %copy.40), calls=%async_computation.3 | async-start | bytes 5242880 | tf_op jit(solution)/shard_map/all_to_all | solution.py:46
  267.0 0.4 fusion.40
  267.4 61.9 %all-to-all-done.3 = bf16[64,16,1,1280]{3,1,2,0:T(8,128)(2,1)S(1)} async-done(((bf16[64,16,1,1280]{3,1,2,0:T(8,128)(2,1)}), bf16[64,16,1,1280]{3,1,2,0:T(8,128)(2,1)S(1)}, u32[]{:S(2)}, u32[]{:S(2)}) %all-to-all-start.3) | async-done | bytes 2621472 | tf_op jit(solution)/shard_map/all_to_all | solution.py:46
  329.3 2.8 copy.41
  332.1 5.1 %reduce_sum.32 = bf16[4,128,1280]{2,0,1:T(4,128)(2,1)} reduce(bf16[4,128,2,1280]{3,0,2,1:T(4,128)(2,1)} %bitcast.49, bf16[]{:T(256)} %constant.8.clone.1), dimensions={2}, to_apply=%region_4.0 | reduce | flops 655360 | bytes 3932162 | tf_op jit(solution)/shard_map/reduce_sum | solution.py:48
  337.2 5.3 %convolution_convert_fusion = bf16[4,256,1280]{2,1,0:T(8,128)(2,1)} fusion(bf16[4,128,1280]{2,0,1:T(4,128)(2,1)} %reduce_sum.32, f32[4,256]{1,0:T(4,128)S(1)} %fusion.40, f32[4,256,128]{2,1,0:T(8,128)} %copy-done.2), kind=kOutput, calls=%fused_computation.13 | convolution fusion | flops 337249408 | bytes 4460544 | tf_op jit(solution)/shard_map/bme,bed->bmd/dot_general | solution.py:49
  (9 shorter events, 0.2 us)
Async XLA Ops:
  0.0 162.2 %copy-start = (bf16[1,1280,1280]{2,1,0:T(8,128)(2,1)S(1)}, bf16[1,1280,1280]{2,1,0:T(8,128)(2,1)}, u32[]{:S(2)}) copy-start(bf16[1,1280,1280]{2,1,0:T(8,128)(2,1)} %param.8) | copy-start | bytes 9830404
  2.8 0.8 copy-start.2
  83.9 72.9 %all-to-all-start.1 = ((bf16[64,16,1,1280]{3,0,2,1:T(8,128)(2,1)}), bf16[64,16,1,1280]{3,0,2,1:T(8,128)(2,1)}, u32[]{:S(2)}, u32[]{:S(2)}) async-start(bf16[64,16,1,1280]{3,0,2,1:T(8,128)(2,1)} %copy.34), calls=%async_computation.1 | async-start | bytes 5242880 | tf_op jit(solution)/shard_map/all_to_all | solution.py:41
  252.0 15.0 %copy-start.3 = (f32[4,256,128]{2,1,0:T(8,128)S(1)}, f32[4,256,128]{2,1,0:T(8,128)}, u32[]{:S(2)}) copy-start(f32[4,256,128]{2,1,0:T(8,128)} %copy-done.2) | copy-start | bytes 1572868
  252.0 77.2 %all-to-all-start.3 = ((bf16[64,16,1,1280]{3,1,2,0:T(8,128)(2,1)}), bf16[64,16,1,1280]{3,1,2,0:T(8,128)(2,1)S(1)}, u32[]{:S(2)}, u32[]{:S(2)}) async-start(bf16[64,16,1,1280]{3,1,2,0:T(8,128)(2,1)} %copy.40), calls=%async_computation.3 | async-start | bytes 5242880 | tf_op jit(solution)/shard_map/all_to_all | solution.py:46
  332.1 10.4 %copy-start.1 = (bf16[1,1280,1280]{2,1,0:T(8,128)(2,1)S(1)}, bf16[1,1280,1280]{2,1,0:T(8,128)(2,1)}, u32[]{:S(2)}) copy-start(bf16[1,1280,1280]{2,1,0:T(8,128)(2,1)} %param.8) | copy-start | bytes 9830404
where the time goes:
time: 343 us; the launch traced here: 342 us
  blocking collectives  127 us (37%)
  waiting for transfers between devices  103 us (30%)
  local copies, waits for them, and re-layouts  53.2 us (16%)
  starting transfers between devices  25.1 us (7%)
  matrix products  23.6 us (7%)
  other arithmetic  10.1 us (3%)
    all_to_all x1, blocking collectives, on_device(): lax.all_to_all(doubled, 'expert', split_axis=2, concat_axis=0, tiled=True)  69.5 us
    all_to_all x1, waiting for transfers between devices, on_device(): lax.all_to_all(returned, 'expert', split_axis=0, concat_axis=2, tiled=True)  61.9 us
    all_to_all x1, blocking collectives, on_device(): lax.all_to_all(partial_value.reshape(-1, 1, 1, width), 'dp', split_axis=0...  57.8 us
    all_to_all x1, waiting for transfers between devices, on_device(): lax.all_to_all(across, 'dp', split_axis=1, concat_axis=0, tiled=True)  41.3 us
    shift_right_arithmetic x6, local copies, waits for them, and re-layouts, unpack_flags(): flags = jnp.right_shift(words[..., None], shifts) & 1  21.5 us
    all_to_all x1, starting transfers between devices, on_device(): lax.all_to_all(returned, 'expert', split_axis=0, concat_axis=2, tiled=True)  15 us
    unnamed x11, local copies, waits for them, and re-layouts  13.1 us
    dot_general x1, matrix products, expert_piece(): jnp.dot(hidden, w_out[0], preferred_element_type=jnp.float32)  11.8 us
  transfers between devices with their start and end apart: 2, of which 2 were waited for; matrix products, arithmetic and copies ran while one was open for 6% of the time, Pallas kernels for 0%

commit v1 on v0

--- a/solution.py
+++ b/solution.py
@@ -25,28 +25,23 @@
     image_count = images.shape[0]
     width = images.shape[2]
     experts = router.shape[1]
-    dp_count = lax.axis_size("dp")
-    expert_count = lax.axis_size("expert")
+    both = ("dp", "expert")
     logits = jnp.einsum("bmd,de->bme", images, router, preferred_element_type=jnp.float32)
     dispatch = jax.nn.softmax(logits, axis=1).astype(jnp.bfloat16)
     combine = jax.nn.softmax(logits, axis=2).astype(jnp.bfloat16)
     slot_values = jnp.einsum(
-        "bme,bmd->bed", dispatch, images, preferred_element_type=jnp.float32
+        "bme,bmd->ebd", dispatch, images, preferred_element_type=jnp.float32
     ).astype(jnp.bfloat16)
     kept_units = unpack_flags(keep_bits[:, 0, :])
-    doubled = jnp.repeat(slot_values, SPLIT, axis=1).reshape(
-        image_count, dp_count, expert_count, width
-    )
-    across = lax.all_to_all(doubled, "expert", split_axis=2, concat_axis=0, tiled=True)
-    arrived = lax.all_to_all(across, "dp", split_axis=1, concat_axis=0, tiled=True)
+    doubled = jnp.repeat(slot_values, SPLIT, axis=0)
+    arrived = lax.all_to_all(doubled, both, split_axis=0, concat_axis=0, tiled=True)
     partial_value = expert_piece(arrived.reshape(-1, width), w_in, w_out, kept_units)
     returned = lax.all_to_all(
-        partial_value.reshape(-1, 1, 1, width), "dp", split_axis=0, concat_axis=1, tiled=True
+        partial_value.reshape(-1, image_count, width), both, split_axis=0, concat_axis=0, tiled=True
     )
-    returned = lax.all_to_all(returned, "expert", split_axis=0, concat_axis=2, tiled=True)
-    paired = returned.reshape(image_count, experts, SPLIT, width)
-    expert_out = paired.astype(jnp.float32).sum(axis=2).astype(jnp.bfloat16)
-    mixed = jnp.einsum("bme,bed->bmd", combine, expert_out, preferred_element_type=jnp.float32)
+    paired = returned.reshape(experts, SPLIT, image_count, width)
+    expert_out = paired.astype(jnp.float32).sum(axis=1).astype(jnp.bfloat16)
+    mixed = jnp.einsum("bme,ebd->bmd", combine, expert_out, preferred_element_type=jnp.float32)
     return mixed.astype(jnp.bfloat16)
 
 

time: 343 us -> 197 us (0.57)
  blocking collectives: 127 us -> 0 us
  local copies, waits for them, and re-layouts: 53.2 us -> 37.6 us
    all_to_all x2 -> x0, blocking collectives: 127 us -> none  [the longest x1 69.5 us: on_device(): lax.all_to_all(doubled, 'expert', split_axis=2, concat_axis=0, tiled=True)]
    all_to_all x6 -> x0, local copies, waits for them, and re-layouts: 13.9 us -> none  [the longest x2 5.45 us: on_device(): lax.all_to_all(across, 'dp', split_axis=1, concat_axis=0, tiled=True)]
    unnamed x11 -> x4, local copies, waits for them, and re-layouts: 13.1 us -> 0.8 us
    reshape x1 -> x2, local copies, waits for them, and re-layouts: 0.51 us -> 10.8 us  [the longest x1 5.53 us: on_device(): partial_value.reshape(-1, image_count, width)]
    reshape x1 -> x0, other arithmetic: 4.45 us -> none  [on_device(): partial_value.reshape(-1, 1, 1, width)]
  transfers between devices with their start and end apart: 2 -> 2, of which waited for: 2 -> 2; matrix products, arithmetic and copies ran while one was open for 6% -> 12% of each run, Pallas kernels for 0% -> 0%
where the time goes in v1:
time: 197 us; the launch traced here: 195 us
  waiting for transfers between devices  102 us (52%)
  local copies, waits for them, and re-layouts  37.6 us (19%)
  starting transfers between devices  25.4 us (13%)
  matrix products  23.6 us (12%)
  other arithmetic  6.82 us (3%)
    all_to_all x1, waiting for transfers between devices, on_device(): lax.all_to_all(partial_value.reshape(-1, image_count, width), both, split...  60.7 us
    all_to_all x1, waiting for transfers between devices, on_device(): lax.all_to_all(doubled, both, split_axis=0, concat_axis=0, tiled=True)  40.8 us
    shift_right_arithmetic x6, local copies, waits for them, and re-layouts, unpack_flags(): flags = jnp.right_shift(words[..., None], shifts) & 1  21.5 us
    all_to_all x1, starting transfers between devices, on_device(): lax.all_to_all(doubled, both, split_axis=0, concat_axis=0, tiled=True)  16.5 us
    dot_general x1, matrix products, expert_piece(): jnp.dot(hidden, w_out[0], preferred_element_type=jnp.float32)  11.8 us
    all_to_all x1, starting transfers between devices, on_device(): lax.all_to_all(partial_value.reshape(-1, image_count, width), both, split...  8.87 us
    reshape x1, local copies, waits for them, and re-layouts, on_device(): partial_value.reshape(-1, image_count, width)  5.53 us
    reshape x1, local copies, waits for them, and re-layouts, on_device(): arrived.reshape(-1, width)  5.31 us
  transfers between devices with their start and end apart: 2, of which 2 were waited for; matrix products, arithmetic and copies ran while one was open for 12% of the time, Pallas kernels for 0%

profile of v1, /device:TPU:1, one launch (start us, length us, event | category | flops | bytes accessed | tf_op | source)
XLA Modules:
  0.0 194.9 jit_solution(6517834149262296365)
XLA Ops:
  0.0 0.0 copy-start
  0.0 2.7 %fusion.25 = f32[4,256,128]{2,1,0:T(8,128)S(1)} fusion(bf16[4,256,1280]{2,1,0:T(8,128)(2,1)} %param.5, bf16[1280,128]{1,0:T(8,128)(2,1)} %param.6), kind=kOutput, calls=%fused_computation.28 | convolution fusion | flops 335544320 | bytes 3473408 | tf_op jit(solution)/shard_map/bmd,de->bme/dot_general | solution.py:29
  2.8 0.0 copy-start.1
  2.8 0.8 copy-done.1
  3.6 0.1 fusion.37
  3.7 3.7 %fusion.17 = bf16[128,4,1280]{2,0,1:T(8,128)(2,1)} fusion(bf16[4,256,1280]{2,1,0:T(8,128)(2,1)} %param.5, f32[4,128]{1,0:T(4,128)S(1)} %fusion.37, f32[4,256,128]{2,1,0:T(8,128)} %copy-done.1), kind=kOutput, calls=%fused_computation.19 | convolution fusion | flops 336593664 | bytes 4458496 | tf_op jit(solution)/shard_map/bme,bmd->ebd/dot_general | solution.py:32
  7.4 2.3 %copy.13 = bf16[128,4,1280]{2,1,0:T(4,128)(2,1)S(1)} copy(bf16[128,4,1280]{2,0,1:T(8,128)(2,1)} %fusion.17) | data formatting | bytes 2621440 | tf_op jit(solution)/shard_map/convert_element_type | solution.py:34
  9.8 2.2 %broadcast_in_dim.2 = bf16[128,2,4,1280]{3,2,1,0:T(4,128)(2,1)} broadcast(bf16[128,4,1280]{2,1,0:T(4,128)(2,1)S(1)} %copy.13), dimensions={0,2,3} | broadcast | bytes 3932160 | tf_op jit(solution)/shard_map/broadcast_in_dim | solution.py:36
  11.9 16.5 %all-to-all-start = ((bf16[256,4,1280]{2,1,0:T(4,128)(2,1)}), bf16[256,4,1280]{2,1,0:T(4,128)(2,1)}, u32[]{:S(2)}, u32[]{:S(2)}) async-start(bf16[256,4,1280]{2,1,0:T(4,128)(2,1)} %bitcast.28), calls=%async_computation | async-start | bytes 5242880 | tf_op jit(solution)/shard_map/all_to_all | solution.py:37
  28.5 2.1 %copy.14 = s32[1024,128]{0,1:T(8,128)} copy(s32[1024,128]{1,0:T(8,128)} %bitcast.29) | data formatting | bytes 1048576 | tf_op jit(solution)/shard_map/shift_right_arithmetic | solution.py:14
  30.6 5.4 %shift_right_arithmetic.23 = s32[1024,128,10]{0,2,1:T(8,128)} broadcast(s32[1024,128]{0,1:T(8,128)} %copy.14), dimensions={0,1} | broadcast | bytes 5767168 | tf_op jit(solution)/shard_map/shift_right_arithmetic | solution.py:14
  35.9 7.9 %shift_right_arithmetic.24 = s32[1024,1280]{0,1:T(8,128)} reshape(s32[1024,128,10]{0,2,1:T(8,128)} %shift_right_arithmetic.23) | data formatting | bytes 10485760 | tf_op jit(solution)/shard_map/shift_right_arithmetic | solution.py:14
  43.9 5.9 %copy.15 = s32[1024,1280]{1,0:T(8,128)} copy(s32[1024,1280]{0,1:T(8,128)} %shift_right_arithmetic.24) | data formatting | bytes 10485760 | tf_op jit(solution)/shard_map/shift_right_arithmetic | solution.py:14
  49.8 0.1 shift_right_arithmetic.26
  49.9 40.8 %all-to-all-done = bf16[256,4,1280]{2,1,0:T(4,128)(2,1)} async-done(((bf16[256,4,1280]{2,1,0:T(4,128)(2,1)}), bf16[256,4,1280]{2,1,0:T(4,128)(2,1)}, u32[]{:S(2)}, u32[]{:S(2)}) %all-to-all-start) | async-done | bytes 2621472 | tf_op jit(solution)/shard_map/all_to_all | solution.py:37
  90.7 5.3 %reshape.21 = bf16[1024,1280]{1,0:T(8,128)(2,1)} reshape(bf16[256,4,1280]{2,1,0:T(4,128)(2,1)} %all-to-all-done) | data formatting | bytes 5242880 | tf_op jit(solution)/shard_map/reshape | solution.py:38
  96.1 0.0 copy-done
  96.1 11.8 %convolution_convert_fusion.1 = bf16[1024,1280]{1,0:T(8,128)(2,1)} fusion(bf16[1,1280,1280]{2,1,0:T(8,128)(2,1)S(1)} %copy-done, s32[1024,1280]{1,0:T(8,128)} %copy.15, bf16[1024,1280]{1,0:T(8,128)(2,1)} %reshape.21, bf16[1,1280,1280]{2,1,0:T(8,128)(2,1)} %param.7, s32[1280]{0:T(1024)S(1)} %shift_right_arithmetic.26), kind=kOutput, calls=%fused_computation.14 | convolution fusion | flops 6730547200 | bytes 17044480 | tf_op jit(solution)/shard_map/dot_general | solution.py:21
  107.9 5.5 %reshape.22 = bf16[256,4,1280]{2,1,0:T(4,128)(2,1)} reshape(bf16[1024,1280]{1,0:T(8,128)(2,1)} %convolution_convert_fusion.1) | data formatting | bytes 5242880 | tf_op jit(solution)/shard_map/reshape | solution.py:40
  113.4 8.9 %all-to-all-start.1 = ((bf16[256,4,1280]{2,1,0:T(4,128)(2,1)}), bf16[256,4,1280]{2,1,0:T(4,128)(2,1)}, u32[]{:S(2)}, u32[]{:S(2)}) async-start(bf16[256,4,1280]{2,1,0:T(4,128)(2,1)} %reshape.22), calls=%async_computation.1 | async-start | bytes 5242880 | tf_op jit(solution)/shard_map/all_to_all | solution.py:39
  122.3 1.6 fusion.38
  123.9 60.7 %all-to-all-done.1 = bf16[256,4,1280]{2,1,0:T(4,128)(2,1)} async-done(((bf16[256,4,1280]{2,1,0:T(4,128)(2,1)}), bf16[256,4,1280]{2,1,0:T(4,128)(2,1)}, u32[]{:S(2)}, u32[]{:S(2)}) %all-to-all-start.1) | async-done | bytes 2621472 | tf_op jit(solution)/shard_map/all_to_all | solution.py:39
  184.6 5.1 %bitcast_reduce_fusion = bf16[128,4,1280]{2,1,0:T(4,128)(2,1)} fusion(bf16[256,4,1280]{2,1,0:T(4,128)(2,1)} %all-to-all-done.1), kind=kLoop, calls=%fused_computation.20 | loop fusion | flops 655360 | bytes 3932160 | tf_op jit(solution)/shard_map/reduce_sum | solution.py:43
  189.7 5.3 %convolution_convert_fusion = bf16[4,256,1280]{2,1,0:T(8,128)(2,1)} fusion(bf16[128,4,1280]{2,1,0:T(4,128)(2,1)} %bitcast_reduce_fusion, f32[4,256]{1,0:T(4,128)S(1)} %fusion.38, f32[4,256,128]{2,1,0:T(8,128)} %copy-done.1), kind=kOutput, calls=%fused_computation.13 | convolution fusion | flops 337249408 | bytes 4460544 | tf_op jit(solution)/shard_map/bme,ebd->bmd/dot_general | solution.py:44
  (1 shorter events, 0.0 us)
Async XLA Ops:
  0.0 96.1 %copy-start = (bf16[1,1280,1280]{2,1,0:T(8,128)(2,1)S(1)}, bf16[1,1280,1280]{2,1,0:T(8,128)(2,1)}, u32[]{:S(2)}) copy-start(bf16[1,1280,1280]{2,1,0:T(8,128)(2,1)} %param.8) | copy-start | bytes 9830404
  2.8 0.8 copy-start.1
  11.9 78.8 %all-to-all-start = ((bf16[256,4,1280]{2,1,0:T(4,128)(2,1)}), bf16[256,4,1280]{2,1,0:T(4,128)(2,1)}, u32[]{:S(2)}, u32[]{:S(2)}) async-start(bf16[256,4,1280]{2,1,0:T(4,128)(2,1)} %bitcast.28), calls=%async_computation | async-start | bytes 5242880 | tf_op jit(solution)/shard_map/all_to_all | solution.py:37
  113.4 71.2 %all-to-all-start.1 = ((bf16[256,4,1280]{2,1,0:T(4,128)(2,1)}), bf16[256,4,1280]{2,1,0:T(4,128)(2,1)}, u32[]{:S(2)}, u32[]{:S(2)}) async-start(bf16[256,4,1280]{2,1,0:T(4,128)(2,1)} %reshape.22), calls=%async_computation.1 | async-start | bytes 5242880 | tf_op jit(solution)/shard_map/all_to_all | solution.py:39

commit v2 on v1

v2 whole, which is shorter than its diff:
```python
import functools

import jax
import jax.numpy as jnp
import numpy as np
from jax import lax
from jax.experimental import pallas as pl
from jax.experimental.pallas import tpu as pltpu
from jax.sharding import PartitionSpec as P

GROUPS = 4
ROWS = 8
PAIRS = 4
IMG = 4
PATCHES = 256
D = 1280
E = 128
IMAGES = 1024
TILE = 256
MESH = pl.DeviceIdType.MESH
KEEP_RATE = 0.875
BF16 = jnp.bfloat16
F32 = jnp.float32


def slot_order():
    table = np.zeros((GROUPS * ROWS * PAIRS * IMG, IMG * E), np.float32)
    for y in range(4):
        for s in range(ROWS):
            for q in range(PAIRS):
                expert = (q // 2) * 64 + y * 16 + (s // 4) * 8 + (s % 4) * 2 + q % 2
                for b in range(IMG):
                    table[((y * ROWS + s) * PAIRS + q) * IMG + b, b * E + expert] = 1.0
    return table


def pair_order():
    table = np.zeros((128, 128), np.float32)
    for q in range(PAIRS):
        for s in range(ROWS):
            for b in range(IMG):
                table[(q * ROWS + s) * IMG + b, (s * PAIRS + q) * IMG + b] = 1.0
    return table


def bit_table():
    table = np.zeros((256, D), np.float32)
    for w in range(128):
        for i in range(10):
            table[w, 10 * w + i] = 32.0 / 2**i
            table[128 + w, 10 * w + i] = 1.0 / 2**i
    return table


def step_along_y(g):
    return g + lax.div(g, 2) * (1 - 2 * lax.rem(g, 2))


def kernel(
    img_h, router_h, w1_h, w2_h, kb_h, order_h, pairs_h, bits_h,
    out_h, spread_h,
    img, router, w1, w2, kb, order, pairs, bits, words, logits, raw, slots,
    xa, za, rows, part, other, total, back, xb, hidden, keep, spread,
    load_sem, xa_send, xa_recv, z_send, z_recv, f_send, f_recv,
    q_send, q_recv, t_send, t_recv, xb_send, xb_recv, out_sem,
):
    dp = lax.axis_index("dp")
    ex = lax.axis_index("expert")
    core = lax.rem(dp, 2)
    y = lax.rem(lax.div(dp, 2), 4)
    z = lax.div(dp, 8) * 4 + lax.rem(ex, 4)
    x = lax.div(ex, 4)
    me = core * 4 + x
    pair = lax.div(z, 2)
    sg = 2 * lax.rem(z, 2) - 1

    def at(s, yy, zz):
        return (
            lax.div(zz, 4) * 8 + yy * 2 + lax.div(s, 4),
            lax.rem(s, 4) * 4 + lax.rem(zz, 4),
        )

    def along_z(step):
        return lax.rem(z + step * sg + 8, 8)

    def along_y(step):
        return lax.rem(y + step + 4, 4)

    loads = [
        (img_h.at[0], img.at[0]),
        (router_h, router),
        (img_h.at[1], img.at[1]),
        (img_h.at[2], img.at[2]),
        (img_h.at[3], img.at[3]),
        (order_h, order),
        (pairs_h, pairs),
        (kb_h, kb),
        (bits_h, bits),
        (w1_h.at[0], w1),
        (w2_h.at[0], w2),
    ]
    copies = [
        pltpu.make_async_copy(src, dst, load_sem.at[i]) for i, (src, dst) in enumerate(loads)
    ]
    for copy in copies:
        copy.start()

    barrier = pltpu.get_barrier_semaphore()
    partners = []
    for dy in range(4):
        for i in range(ROWS):
            if dy or i:
                partners.append(at(lax.rem(me + i, ROWS), along_y(dy), z))
    for step in (1, 2, 3, -1, -2):
        partners.append(at(me, y, along_z(step)))
    for partner in partners:
        pl.semaphore_signal(barrier, inc=1, device_id=partner, device_id_type=MESH)

    for b in range(IMG):
        if b == 0:
            copies[0].wait()
            copies[1].wait()
        else:
            copies[1 + b].wait()
        scores = jnp.dot(img[b], router[...], preferred_element_type=F32)
        logits[b] = scores
        top = jnp.max(scores, axis=0, keepdims=True)
        grown = jnp.exp(scores - top)
        share = (grown / jnp.sum(grown, axis=0, keepdims=True)).astype(BF16)
        for n in range(D // TILE):
            cols = pl.ds(n * TILE, TILE)
            raw[pl.ds(b * E, E), cols] = lax.dot_general(
                share, img[b, :, cols], (((0,), (0,)), ((), ())), preferred_element_type=F32
            ).astype(BF16)

    copies[5].wait()
    for g in range(GROUPS):
        dy = (0, 1, 3, 2)[g]
        yy = along_y(dy)
        pick = order[pl.ds(pl.multiple_of(yy * 128, 128), 128), :]
        for n in range(D // TILE):
            cols = pl.ds(n * TILE, TILE)
            slots[g, :, :, cols] = (
                jnp.dot(pick, raw[:, cols], preferred_element_type=F32)
                .astype(BF16)
                .reshape(ROWS, 16, TILE)
            )
        if g == 0:
            pl.semaphore_wait(barrier, len(partners))
        for i in range(ROWS):
            s = lax.rem(me + i, ROWS)
            if g == 0 and i == 0:
                pltpu.make_async_copy(slots.at[g, s], xa.at[g, me], xa_recv.at[g]).start()
            else:
                pltpu.make_async_remote_copy(
                    slots.at[g, s], xa.at[g, me], xa_send.at[g], xa_recv.at[g],
                    device_id=at(s, yy, z), device_id_type=MESH,
                ).start()

    for b in range(IMG):
        scores = logits[b]
        grown = jnp.exp(scores - jnp.max(scores, axis=1, keepdims=True))
        share = (grown / jnp.sum(grown, axis=1, keepdims=True)).astype(BF16)
        spread[pl.ds(b * PATCHES, PATCHES), :] = lax.dot_general(
            share, order[:, pl.ds(b * E, E)], (((1,), (1,)), ((), ())), preferred_element_type=F32
        ).astype(BF16)
    spread_out = pltpu.make_async_copy(spread, spread_h, out_sem)
    spread_out.start()

    copies[7].wait()
    words[:, pl.ds(0, 128)] = jnp.right_shift(kb[...], 5).astype(F32).astype(BF16)
    words[:, pl.ds(128, 128)] = jnp.bitwise_and(kb[...], 31).astype(F32).astype(BF16)
    for i in (6, 8, 9, 10):
        copies[i].wait()

    def arrived(ref, sem):
        pltpu.make_async_copy(ref, ref, sem).wait()

    def send(src, dst, send_sem, recv_sem, zz):
        pltpu.make_async_remote_copy(
            src, dst, send_sem, recv_sem, device_id=at(me, y, zz), device_id_type=MESH
        ).start()

    def dispatch(g):
        arrived(xa.at[g], xa_recv.at[g])
        for n in range(D // TILE):
            cols = pl.ds(n * TILE, TILE)
            za[g, :, :, cols] = (
                jnp.dot(
                    pairs[...], xa[g, :, :, cols].reshape(128, TILE), preferred_element_type=F32
                )
                .astype(BF16)
                .reshape(PAIRS, 32, TILE)
            )
        send(za.at[g, pair], rows.at[g, 4], z_send.at[g, 0], z_recv.at[g, 0], along_z(-1))
        for slot, step in ((3, 3), (2, -2), (1, 1)):
            zz = along_z(step)
            send(
                za.at[g, lax.div(zz, 2)], rows.at[g, slot],
                z_send.at[g, slot], z_recv.at[g, slot], zz,
            )
        rows[g, 0] = za[g, pair]

    def keep_flags(g):
        r = lax.broadcasted_iota(jnp.int32, (256, 1), 0)
        j = jnp.right_shift(r, 5)
        s = jnp.bitwise_and(jnp.right_shift(r, 2), 7)
        zz = jnp.bitwise_and(jnp.where(j < 4, z + j * sg, z - (j - 3) * sg) + 8, 7)
        yy = along_y(-step_along_y(g))
        group = (jnp.right_shift(zz, 2) * 8 + yy * 2 + jnp.right_shift(s, 2)) * 16
        device = group + jnp.bitwise_and(s, 3) * 4 + jnp.bitwise_and(zz, 3)
        image = device * IMG + jnp.bitwise_and(r, 3)
        c = lax.broadcasted_iota(jnp.int32, (256, IMAGES), 1)
        pick = jnp.where(c == image, 1.0, 0.0).astype(BF16)
        mine = jnp.dot(pick, words[...], preferred_element_type=F32).astype(BF16)

        def tile(n, carry):
            cols = pl.ds(pl.multiple_of(n * TILE, TILE), TILE)
            value = jnp.dot(mine, bits[:, cols], preferred_element_type=F32)
            flag = jnp.bitwise_and(value.astype(jnp.int32), 1)
            keep[:, cols] = flag.astype(F32).astype(BF16)
            return carry

        lax.fori_loop(0, D // TILE, tile, 0)

    def forward(g):
        for j in (3, 2, 1):
            arrived(rows.at[g, j], z_recv.at[g, j])
            send(
                rows.at[g, j], rows.at[g, 4 + j], f_send.at[g, j], f_recv.at[g, j], along_z(-1)
            )

    def experts(g):
        keep_flags(g)
        arrived(rows.at[g, 4], z_recv.at[g, 0])
        for j in (1, 2, 3):
            arrived(rows.at[g, 4 + j], f_recv.at[g, j])

        def first(n, carry):
            cols = pl.ds(pl.multiple_of(n * TILE, TILE), TILE)
            value = jnp.dot(rows[g].reshape(256, D), w1[:, cols], preferred_element_type=F32)
            flag = keep[:, cols].astype(F32)
            hidden[:, cols] = (jax.nn.gelu(value) * flag * (1.0 / KEEP_RATE)).astype(BF16)
            return carry

        def second(n, carry):
            cols = pl.ds(pl.multiple_of(n * TILE, TILE), TILE)
            value = jnp.dot(hidden[...], w2[:, cols], preferred_element_type=F32)
            part[g, :, :, cols] = value.astype(BF16).reshape(8, 32, TILE)
            return carry

        lax.fori_loop(0, D // TILE, first, 0)
        lax.fori_loop(0, D // TILE, second, 0)
        for j in (3, 2, 1, 0):
            send(
                part.at[g, 4 + j], other.at[g, j], q_send.at[g, j], q_recv.at[g, j], along_z(-1)
            )

    def gather_pair(g):
        for j in (3, 2, 1, 0):
            arrived(other.at[g, j], q_recv.at[g, j])
            value = (part[g, j].astype(F32) + other[g, j].astype(F32)).astype(BF16)
            if j == 0:
                back[g, pair] = value
            else:
                total[g, j] = value
                send(
                    total.at[g, j], back.at[g, pair],
                    t_send.at[g, j], t_recv.at[g, j], along_z(j),
                )

    def give_back(g):
        for slot, step in ((1, 1), (2, -2), (3, 3)):
            arrived(back.at[g, lax.div(along_z(step), 2)], t_recv.at[g, slot])
        for n in range(D // TILE):
            cols = pl.ds(n * TILE, TILE)
            xb[g, :, :, cols] = (
                lax.dot_general(
                    pairs[...], back[g, :, :, cols].reshape(128, TILE),
                    (((0,), (0,)), ((), ())), preferred_element_type=F32,
                )
                .astype(BF16)
                .reshape(ROWS, 16, TILE)
            )
        yy = along_y(-step_along_y(g))
        for i in range(ROWS):
            s = lax.rem(me + i, ROWS)

            def start_remote(s=s):
                pltpu.make_async_remote_copy(
                    xb.at[g, s], out_h.at[y, me], xb_send.at[g], xb_recv.at[g],
                    device_id=at(s, yy, z), device_id_type=MESH,
                ).start()

            if i:
                start_remote()
            else:

                @pl.when(g == 0)
                def _():
                    pltpu.make_async_copy(xb.at[g, me], out_h.at[y, me], xb_recv.at[g]).start()

                pl.when(g > 0)(start_remote)

    stages = (dispatch, forward, experts, gather_pair, give_back)

    def turn(t, carry):
        for lag, stage in enumerate(stages):
            g = t - lag
            pl.when(jnp.logical_and(g >= 0, g < GROUPS))(functools.partial(stage, g))
        return carry

    lax.fori_loop(0, GROUPS + len(stages) - 1, turn, 0)

    spread_out.wait()
    for g in range(GROUPS):
        first_row = 1 if g == 0 else 0
        remote = pl.ds(first_row, ROWS - first_row)
        arrived(slots.at[g, remote], xa_send.at[g])
        for slot in range(4):
            arrived(za.at[g, slot], z_send.at[g, slot])
            arrived(part.at[g, 4 + slot], q_send.at[g, slot])
            if slot:
                arrived(rows.at[g, slot], f_send.at[g, slot])
                arrived(total.at[g, slot], t_send.at[g, slot])
        arrived(xb.at[g, remote], xb_send.at[g])
        arrived(out_h.at[along_y((0, 1, 3, 2)[g])], xb_recv.at[g])


def exchange(images, router, w_in, w_out, words):
    order = jnp.asarray(slot_order(), BF16)
    pairs = jnp.asarray(pair_order(), BF16)
    bits = jnp.asarray(bit_table(), BF16)
    anywhere = pl.BlockSpec(memory_space=pl.ANY)
    dma = pltpu.SemaphoreType.DMA
    return pl.pallas_call(
        kernel,
        out_shape=(
            jax.ShapeDtypeStruct((GROUPS, ROWS, 16, D), BF16),
            jax.ShapeDtypeStruct((IMG * PATCHES, IMG * E), BF16),
        ),
        in_specs=[anywhere] * 8,
        out_specs=(anywhere, anywhere),
        scratch_shapes=[
            pltpu.VMEM((IMG, PATCHES, D), BF16),
            pltpu.VMEM((D, E), BF16),
            pltpu.VMEM((D, D), BF16),
            pltpu.VMEM((D, D), BF16),
            pltpu.VMEM((IMAGES, 128), jnp.int32),
            pltpu.VMEM((512, 512), BF16),
            pltpu.VMEM((128, 128), BF16),
            pltpu.VMEM((256, D), BF16),
            pltpu.VMEM((IMAGES, 256), BF16),
            pltpu.VMEM((IMG, PATCHES, E), F32),
            pltpu.VMEM((IMG * E, D), BF16),
            pltpu.VMEM((GROUPS, ROWS, 16, D), BF16),
            pltpu.VMEM((GROUPS, ROWS, 16, D), BF16),
            pltpu.VMEM((GROUPS, PAIRS, 32, D), BF16),
            pltpu.VMEM((GROUPS, 8, 32, D), BF16),
            pltpu.VMEM((GROUPS, 8, 32, D), BF16),
            pltpu.VMEM((GROUPS, 4, 32, D), BF16),
            pltpu.VMEM((GROUPS, 4, 32, D), BF16),
            pltpu.VMEM((GROUPS, PAIRS, 32, D), BF16),
            pltpu.VMEM((GROUPS, ROWS, 16, D), BF16),
            pltpu.VMEM((256, D), BF16),
            pltpu.VMEM((256, D), BF16),
            pltpu.VMEM((IMG * PATCHES, IMG * E), BF16),
            dma((11,)),
            dma((4,)), dma((4,)),
            dma((4, 4)), dma((4, 4)),
            dma((4, 4)), dma((4, 4)),
            dma((4, 4)), dma((4, 4)),
            dma((4, 4)), dma((4, 4)),
            dma((4,)), dma((4,)),
            dma,
        ],
        compiler_params=pltpu.CompilerParams(
            collective_id=0, has_side_effects=True, vmem_limit_bytes=60 * 2**20
        ),
    )(images, router, w_in, w_out, words, order, pairs, bits)


def on_device(images, router, w_in, w_out, keep_bits):
    words = keep_bits.reshape(IMAGES, 128)
    arrived, spread = exchange(images, router, w_in, w_out, words)
    mixed = jnp.dot(spread, arrived.reshape(512, D), preferred_element_type=F32)
    return mixed.astype(BF16).reshape(IMG, PATCHES, D)


def solution(mesh):
    placed = (
        P(("dp", "expert"), None, None),
        P(),
        P(("dp", "expert"), None, None),
        P(("dp", "expert"), None, None),
        P(None, ("dp", "expert"), None),
    )
    return jax.shard_map(
        on_device,
        mesh=mesh,
        in_specs=placed,
        out_specs=P(("dp", "expert"), None, None),
        check_vma=False,
    )
```

time: 197 us -> 123 us (0.62); the launches traced: 195 us -> 123 us
  Pallas kernels: 0 us -> 118 us
  waiting for transfers between devices: 102 us -> 0 us
  local copies, waits for them, and re-layouts: 37.6 us -> 0 us
  starting transfers between devices: 25.4 us -> 0 us
  matrix products: 23.6 us -> 4.65 us
  other arithmetic: 6.82 us -> 0 us
    pallas_call x0 -> x1, Pallas kernels: none -> 118 us  [exchange(): pl.pallas_call(kernel, out_shape=(jax.ShapeDtypeStruct((GROUPS, ROWS, 16,...]
    all_to_all x2 -> x0, waiting for transfers between devices: 102 us -> none  [the longest x1 60.7 us: on_device(): lax.all_to_all(partial_value.reshape(-1, image_count, width), both, split...]
    all_to_all x2 -> x0, starting transfers between devices: 25.4 us -> none  [the longest x1 16.5 us: on_device(): lax.all_to_all(doubled, both, split_axis=0, concat_axis=0, tiled=True)]
    shift_right_arithmetic x6 -> x0, local copies, waits for them, and re-layouts: 21.5 us -> none  [unpack_flags(): flags = jnp.right_shift(words[..., None], shifts) & 1]
    dot_general x4 -> x1, matrix products: 23.6 us -> 4.65 us  [on_device(): mixed = jnp.dot(spread, arrived.reshape(512, D), preferred_element_type=F32)]
    reshape x2 -> x0, local copies, waits for them, and re-layouts: 10.8 us -> none  [the longest x1 5.53 us: on_device(): partial_value.reshape(-1, image_count, width)]
    reduce_sum x1 -> x0, other arithmetic: 5.1 us -> none  [on_device(): expert_out = paired.astype(jnp.float32).sum(axis=1).astype(jnp.bfloat16)]
    convert_element_type x1 -> x0, local copies, waits for them, and re-layouts: 2.33 us -> none  [on_device(): slot_values = jnp.einsum('bme,bmd->ebd', dispatch, images, preferred_elem...]
  transfers between devices with their start and end apart: 2 -> 0, of which waited for: 2 -> 0; matrix products, arithmetic and copies ran while one was open for 12% -> 0% of each run, Pallas kernels for 0% -> 0%
where the time goes in v2:
time: 123 us
  Pallas kernels  118 us (96%)
  matrix products  4.65 us (4%)
    pallas_call x1, Pallas kernels, exchange(): pl.pallas_call(kernel, out_shape=(jax.ShapeDtypeStruct((GROUPS, ROWS, 16,...  118 us
    dot_general x1, matrix products, on_device(): mixed = jnp.dot(spread, arrived.reshape(512, D), preferred_element_type=F32)  4.65 us

profile of v2, /device:TPU:1, one launch (start us, length us, event | category | flops | bytes accessed | tf_op | source)
XLA Modules:
  0.0 123.1 jit_solution(240829529619394638)
XLA Ops:
  0.0 118.4 %shard_map.82 = (bf16[4,8,16,1280]{3,2,1,0:T(8,128)(2,1)}, bf16[1024,512]{1,0:T(8,128)(2,1)}) custom-call(bf16[4,256,1280]{2,1,0:T(8,128)(2,1)} %img_h.1, bf16[1280,128]{1,0:T(8,128)(2,1)} %router_h.1, bf16[1,1280,1280]{2,1,0:T(8,128)(2,1)} %w1_h.1, bf16[1,1280,1280]{2,1,0:T(8,128)(2,1)} %w2_h.1, s32[1024,128]{1,0:T(8,128)} %bitcast.5, ...), custom_call_target="tpu_custom_call" | custom-call | tf_op jit(solution)/shard_map/pallas_call | solution.py:336
  118.4 4.7 %convolution_convert_fusion = bf16[1024,1280]{1,0:T(8,128)(2,1)} fusion(bf16[1024,512]{1,0:T(8,128)(2,1)} %get-tuple-element.7, bf16[512,1280]{1,0:T(8,128)(2,1)} %bitcast.6), kind=kOutput, calls=%fused_computation | convolution fusion | flops 1343488000 | bytes 4980736 | tf_op jit(solution)/shard_map/dot_general | solution.py:386

commit v3 on v2

--- a/solution.py
+++ b/solution.py
@@ -8,8 +8,13 @@
 from jax.experimental.pallas import tpu as pltpu
 from jax.sharding import PartitionSpec as P
 
-GROUPS = 4
-ROWS = 8
+GROUPS = 8
+PLANE = 32
+UNITS = 4
+OFFSETS = (
+    (0, 0), (1, 0), (0, 1), (1, 1), (2, 0), (1, 3), (2, 2), (0, 2),
+    (2, 1), (2, 3), (1, 2), (3, 2), (3, 1), (3, 3), (3, 0), (0, 3),
+)
 PAIRS = 4
 IMG = 4
 PATCHES = 256
@@ -24,22 +29,22 @@
 
 
 def slot_order():
-    table = np.zeros((GROUPS * ROWS * PAIRS * IMG, IMG * E), np.float32)
-    for y in range(4):
-        for s in range(ROWS):
-            for q in range(PAIRS):
-                expert = (q // 2) * 64 + y * 16 + (s // 4) * 8 + (s % 4) * 2 + q % 2
-                for b in range(IMG):
-                    table[((y * ROWS + s) * PAIRS + q) * IMG + b, b * E + expert] = 1.0
+    table = np.zeros((PLANE * PAIRS * IMG, IMG * E), np.float32)
+    for s in range(PLANE):
+        for q in range(PAIRS):
+            local = (s // 8) * 16 + (s % 2) * 8 + (s // 2 % 4) * 2
+            expert = (q // 2) * 64 + local + q % 2
+            for b in range(IMG):
+                table[(s * PAIRS + q) * IMG + b, b * E + expert] = 1.0
     return table
 
 
 def pair_order():
-    table = np.zeros((128, 128), np.float32)
+    table = np.zeros((64, 64), np.float32)
     for q in range(PAIRS):
-        for s in range(ROWS):
+        for u in range(UNITS):
             for b in range(IMG):
-                table[(q * ROWS + s) * IMG + b, (s * PAIRS + q) * IMG + b] = 1.0
+                table[(q * UNITS + u) * IMG + b, (u * PAIRS + q) * IMG + b] = 1.0
     return table
 
 
@@ -52,8 +57,15 @@
     return table
 
 
-def step_along_y(g):
-    return g + lax.div(g, 2) * (1 - 2 * lax.rem(g, 2))
+def offset(g, chip):
+    if isinstance(g, int):
+        return OFFSETS[2 * g + chip]
+    dx, dy = OFFSETS[chip]
+    for i in range(1, GROUPS):
+        here = g == i
+        dx = jnp.where(here, OFFSETS[2 * i + chip][0], dx)
+        dy = jnp.where(here, OFFSETS[2 * i + chip][1], dy)
+    return dx, dy
 
 
 def kernel(
@@ -70,21 +82,26 @@
     y = lax.rem(lax.div(dp, 2), 4)
     z = lax.div(dp, 8) * 4 + lax.rem(ex, 4)
     x = lax.div(ex, 4)
-    me = core * 4 + x
+    me = (y * 4 + x) * 2 + core
     pair = lax.div(z, 2)
     sg = 2 * lax.rem(z, 2) - 1
 
-    def at(s, yy, zz):
+    def at(s, zz):
         return (
-            lax.div(zz, 4) * 8 + yy * 2 + lax.div(s, 4),
-            lax.rem(s, 4) * 4 + lax.rem(zz, 4),
+            lax.div(zz, 4) * 8 + lax.div(s, 8) * 2 + lax.rem(s, 2),
+            lax.rem(lax.div(s, 2), 4) * 4 + lax.rem(zz, 4),
         )
 
     def along_z(step):
         return lax.rem(z + step * sg + 8, 8)
 
-    def along_y(step):
-        return lax.rem(y + step + 4, 4)
+    def chip_at(g, chip, sign):
+        dx, dy = offset(g, chip)
+        return lax.rem(y + sign * dy + 4, 4) * 4 + lax.rem(x + sign * dx + 4, 4)
+
+    def device_at(g, unit, sign):
+        side = core if unit % 2 == 0 else 1 - core
+        return chip_at(g, unit // 2, sign) * 2 + side
 
     loads = [
         (img_h.at[0], img.at[0]),
@@ -107,12 +124,12 @@
 
     barrier = pltpu.get_barrier_semaphore()
     partners = []
-    for dy in range(4):
-        for i in range(ROWS):
-            if dy or i:
-                partners.append(at(lax.rem(me + i, ROWS), along_y(dy), z))
+    for g in range(GROUPS):
+        for u in range(UNITS):
+            if g or u:
+                partners.append(at(device_at(g, u, 1), z))
     for step in (1, 2, 3, -1, -2):
-        partners.append(at(me, y, along_z(step)))
+        partners.append(at(me, along_z(step)))
     for partner in partners:
         pl.semaphore_signal(barrier, inc=1, device_id=partner, device_id_type=MESH)
 
@@ -134,27 +151,24 @@
             ).astype(BF16)
 
     copies[5].wait()
+    for n in range(D // TILE):
+        cols = pl.ds(n * TILE, TILE)
+        slots[:, :, cols] = (
+            jnp.dot(order[...], raw[:, cols], preferred_element_type=F32)
+            .astype(BF16)
+            .reshape(PLANE, 16, TILE)
+        )
+    pl.semaphore_wait(barrier, len(partners))
     for g in range(GROUPS):
-        dy = (0, 1, 3, 2)[g]
-        yy = along_y(dy)
-        pick = order[pl.ds(pl.multiple_of(yy * 128, 128), 128), :]
-        for n in range(D // TILE):
-            cols = pl.ds(n * TILE, TILE)
-            slots[g, :, :, cols] = (
-                jnp.dot(pick, raw[:, cols], preferred_element_type=F32)
-                .astype(BF16)
-                .reshape(ROWS, 16, TILE)
-            )
-        if g == 0:
-            pl.semaphore_wait(barrier, len(partners))
-        for i in range(ROWS):
-            s = lax.rem(me + i, ROWS)
-            if g == 0 and i == 0:
-                pltpu.make_async_copy(slots.at[g, s], xa.at[g, me], xa_recv.at[g]).start()
+        for u in range(UNITS):
+            s = device_at(g, u, 1)
+            land = xa.at[g, (u // 2) * 2 + core]
+            if g == 0 and u == 0:
+                pltpu.make_async_copy(slots.at[s], land, xa_recv.at[g]).start()
             else:
                 pltpu.make_async_remote_copy(
-                    slots.at[g, s], xa.at[g, me], xa_send.at[g], xa_recv.at[g],
-                    device_id=at(s, yy, z), device_id_type=MESH,
+                    slots.at[s], land, xa_send.at[g], xa_recv.at[g],
+                    device_id=at(s, z), device_id_type=MESH,
                 ).start()
 
     for b in range(IMG):
@@ -178,7 +192,7 @@
 
     def send(src, dst, send_sem, recv_sem, zz):
         pltpu.make_async_remote_copy(
-            src, dst, send_sem, recv_sem, device_id=at(me, y, zz), device_id_type=MESH
+            src, dst, send_sem, recv_sem, device_id=at(me, zz), device_id_type=MESH
         ).start()
 
     def dispatch(g):
@@ -187,10 +201,10 @@
             cols = pl.ds(n * TILE, TILE)
             za[g, :, :, cols] = (
                 jnp.dot(
-                    pairs[...], xa[g, :, :, cols].reshape(128, TILE), preferred_element_type=F32
+                    pairs[...], xa[g, :, :, cols].reshape(64, TILE), preferred_element_type=F32
                 )
                 .astype(BF16)
-                .reshape(PAIRS, 32, TILE)
+                .reshape(PAIRS, 16, TILE)
             )
         send(za.at[g, pair], rows.at[g, 4], z_send.at[g, 0], z_recv.at[g, 0], along_z(-1))
         for slot, step in ((3, 3), (2, -2), (1, 1)):
@@ -202,15 +216,16 @@
         rows[g, 0] = za[g, pair]
 
     def keep_flags(g):
-        r = lax.broadcasted_iota(jnp.int32, (256, 1), 0)
-        j = jnp.right_shift(r, 5)
-        s = jnp.bitwise_and(jnp.right_shift(r, 2), 7)
+        r = lax.broadcasted_iota(jnp.int32, (128, 1), 0)
+        j = jnp.right_shift(r, 4)
+        side = jnp.bitwise_and(jnp.right_shift(r, 2), 1)
         zz = jnp.bitwise_and(jnp.where(j < 4, z + j * sg, z - (j - 3) * sg) + 8, 7)
-        yy = along_y(-step_along_y(g))
-        group = (jnp.right_shift(zz, 2) * 8 + yy * 2 + jnp.right_shift(s, 2)) * 16
-        device = group + jnp.bitwise_and(s, 3) * 4 + jnp.bitwise_and(zz, 3)
+        near, far = chip_at(g, 0, -1), chip_at(g, 1, -1)
+        chip = jnp.where(jnp.bitwise_and(r, 8) == 0, near, far)
+        group = jnp.right_shift(zz, 2) * 8 + jnp.right_shift(chip, 2) * 2 + side
+        device = group * 16 + jnp.bitwise_and(chip, 3) * 4 + jnp.bitwise_and(zz, 3)
         image = device * IMG + jnp.bitwise_and(r, 3)
-        c = lax.broadcasted_iota(jnp.int32, (256, IMAGES), 1)
+        c = lax.broadcasted_iota(jnp.int32, (128, IMAGES), 1)
         pick = jnp.where(c == image, 1.0, 0.0).astype(BF16)
         mine = jnp.dot(pick, words[...], preferred_element_type=F32).astype(BF16)
 
@@ -238,7 +253,7 @@
 
         def first(n, carry):
             cols = pl.ds(pl.multiple_of(n * TILE, TILE), TILE)
-            value = jnp.dot(rows[g].reshape(256, D), w1[:, cols], preferred_element_type=F32)
+            value = jnp.dot(rows[g].reshape(128, D), w1[:, cols], preferred_element_type=F32)
             flag = keep[:, cols].astype(F32)
             hidden[:, cols] = (jax.nn.gelu(value) * flag * (1.0 / KEEP_RATE)).astype(BF16)
             return carry
@@ -246,7 +261,7 @@
         def second(n, carry):
             cols = pl.ds(pl.multiple_of(n * TILE, TILE), TILE)
             value = jnp.dot(hidden[...], w2[:, cols], preferred_element_type=F32)
-            part[g, :, :, cols] = value.astype(BF16).reshape(8, 32, TILE)
+            part[g, :, :, cols] = value.astype(BF16).reshape(8, 16, TILE)
             return carry
 
         lax.fori_loop(0, D // TILE, first, 0)
@@ -276,29 +291,30 @@
             cols = pl.ds(n * TILE, TILE)
             xb[g, :, :, cols] = (
                 lax.dot_general(
-                    pairs[...], back[g, :, :, cols].reshape(128, TILE),
+                    pairs[...], back[g, :, :, cols].reshape(64, TILE),
                     (((0,), (0,)), ((), ())), preferred_element_type=F32,
                 )
                 .astype(BF16)
-                .reshape(ROWS, 16, TILE)
+                .reshape(UNITS, 16, TILE)
             )
-        yy = along_y(-step_along_y(g))
-        for i in range(ROWS):
-            s = lax.rem(me + i, ROWS)
-
-            def start_remote(s=s):
+        for u in range(UNITS):
+            s = device_at(g, u, -1)
+            gone = xb.at[g, (u // 2) * 2 + (core if u % 2 == 0 else 1 - core)]
+            land = xb_recv.at[g, u // 2]
+
+            def start_remote(s=s, gone=gone, land=land):
                 pltpu.make_async_remote_copy(
-                    xb.at[g, s], out_h.at[y, me], xb_send.at[g], xb_recv.at[g],
-                    device_id=at(s, yy, z), device_id_type=MESH,
+                    gone, out_h.at[me], xb_send.at[g], land,
+                    device_id=at(s, z), device_id_type=MESH,
                 ).start()
 
-            if i:
+            if u:
                 start_remote()
             else:
 
                 @pl.when(g == 0)
-                def _():
-                    pltpu.make_async_copy(xb.at[g, me], out_h.at[y, me], xb_recv.at[g]).start()
+                def _(gone=gone, land=land):
+                    pltpu.make_async_copy(gone, out_h.at[me], land).start()
 
                 pl.when(g > 0)(start_remote)
 
@@ -314,9 +330,8 @@
 
     spread_out.wait()
     for g in range(GROUPS):
-        first_row = 1 if g == 0 else 0
-        remote = pl.ds(first_row, ROWS - first_row)
-        arrived(slots.at[g, remote], xa_send.at[g])
+        remote = pl.ds(1, UNITS - 1) if g == 0 else pl.ds(0, UNITS)
+        arrived(xa.at[g, remote], xa_send.at[g])
         for slot in range(4):
             arrived(za.at[g, slot], z_send.at[g, slot])
             arrived(part.at[g, 4 + slot], q_send.at[g, slot])
@@ -324,7 +339,8 @@
                 arrived(rows.at[g, slot], f_send.at[g, slot])
                 arrived(total.at[g, slot], t_send.at[g, slot])
         arrived(xb.at[g, remote], xb_send.at[g])
-        arrived(out_h.at[along_y((0, 1, 3, 2)[g])], xb_recv.at[g])
+        for chip in range(2):
+            arrived(out_h.at[pl.ds(chip_at(g, chip, 1) * 2, 2)], xb_recv.at[g, chip])
 
 
 def exchange(images, router, w_in, w_out, words):
@@ -336,7 +352,7 @@
     return pl.pallas_call(
         kernel,
         out_shape=(
-            jax.ShapeDtypeStruct((GROUPS, ROWS, 16, D), BF16),
+            jax.ShapeDtypeStruct((PLANE, 16, D), BF16),
             jax.ShapeDtypeStruct((IMG * PATCHES, IMG * E), BF16),
         ),
         in_specs=[anywhere] * 8,
@@ -348,30 +364,30 @@
             pltpu.VMEM((D, D), BF16),
             pltpu.VMEM((IMAGES, 128), jnp.int32),
             pltpu.VMEM((512, 512), BF16),
-            pltpu.VMEM((128, 128), BF16),
+            pltpu.VMEM((64, 64), BF16),
             pltpu.VMEM((256, D), BF16),
             pltpu.VMEM((IMAGES, 256), BF16),
             pltpu.VMEM((IMG, PATCHES, E), F32),
             pltpu.VMEM((IMG * E, D), BF16),
-            pltpu.VMEM((GROUPS, ROWS, 16, D), BF16),
-            pltpu.VMEM((GROUPS, ROWS, 16, D), BF16),
-            pltpu.VMEM((GROUPS, PAIRS, 32, D), BF16),
-            pltpu.VMEM((GROUPS, 8, 32, D), BF16),
-            pltpu.VMEM((GROUPS, 8, 32, D), BF16),
-            pltpu.VMEM((GROUPS, 4, 32, D), BF16),
-            pltpu.VMEM((GROUPS, 4, 32, D), BF16),
-            pltpu.VMEM((GROUPS, PAIRS, 32, D), BF16),
-            pltpu.VMEM((GROUPS, ROWS, 16, D), BF16),
-            pltpu.VMEM((256, D), BF16),
-            pltpu.VMEM((256, D), BF16),
+            pltpu.VMEM((PLANE, 16, D), BF16),
+            pltpu.VMEM((GROUPS, UNITS, 16, D), BF16),
+            pltpu.VMEM((GROUPS, PAIRS, 16, D), BF16),
+            pltpu.VMEM((GROUPS, 8, 16, D), BF16),
+            pltpu.VMEM((GROUPS, 8, 16, D), BF16),
+            pltpu.VMEM((GROUPS, 4, 16, D), BF16),
+            pltpu.VMEM((GROUPS, 4, 16, D), BF16),
+            pltpu.VMEM((GROUPS, PAIRS, 16, D), BF16),
+            pltpu.VMEM((GROUPS, UNITS, 16, D), BF16),
+            pltpu.VMEM((128, D), BF16),
+            pltpu.VMEM((128, D), BF16),
             pltpu.VMEM((IMG * PATCHES, IMG * E), BF16),
             dma((11,)),
-            dma((4,)), dma((4,)),
-            dma((4, 4)), dma((4, 4)),
-            dma((4, 4)), dma((4, 4)),
-            dma((4, 4)), dma((4, 4)),
-            dma((4, 4)), dma((4, 4)),
-            dma((4,)), dma((4,)),
+            dma((GROUPS,)), dma((GROUPS,)),
+            dma((GROUPS, 4)), dma((GROUPS, 4)),
+            dma((GROUPS, 4)), dma((GROUPS, 4)),
+            dma((GROUPS, 4)), dma((GROUPS, 4)),
+            dma((GROUPS, 4)), dma((GROUPS, 4)),
+            dma((GROUPS,)), dma((GROUPS, 2)),
             dma,
         ],
         compiler_params=pltpu.CompilerParams(

time: 123 us -> 123 us (level)
  no operation moved by 1% of the time
where the time goes in v3:
time: 123 us; the launch traced here: 122 us
  Pallas kernels  118 us (96%)
  matrix products  4.65 us (4%)
    pallas_call x1, Pallas kernels, exchange(): pl.pallas_call(kernel, out_shape=(jax.ShapeDtypeStruct((PLANE, 16, D), BF...  118 us
    dot_general x1, matrix products, on_device(): mixed = jnp.dot(spread, arrived.reshape(512, D), preferred_element_type=F32)  4.65 us

profile of v3, /device:TPU:1, one launch (start us, length us, event | category | flops | bytes accessed | tf_op | source)
XLA Modules:
  0.0 122.4 jit_solution(8108826330005519663)
XLA Ops:
  0.0 117.8 %shard_map.82 = (bf16[32,16,1280]{2,1,0:T(8,128)(2,1)}, bf16[1024,512]{1,0:T(8,128)(2,1)}) custom-call(bf16[4,256,1280]{2,1,0:T(8,128)(2,1)} %img_h.1, bf16[1280,128]{1,0:T(8,128)(2,1)} %router_h.1, bf16[1,1280,1280]{2,1,0:T(8,128)(2,1)} %w1_h.1, bf16[1,1280,1280]{2,1,0:T(8,128)(2,1)} %w2_h.1, s32[1024,128]{1,0:T(8,128)} %bitcast.5, ...), custom_call_target="tpu_custom_call" | custom-call | tf_op jit(solution)/shard_map/pallas_call | solution.py:352
  117.8 4.7 %convolution_convert_fusion = bf16[1024,1280]{1,0:T(8,128)(2,1)} fusion(bf16[1024,512]{1,0:T(8,128)(2,1)} %get-tuple-element.7, bf16[512,1280]{1,0:T(8,128)(2,1)} %bitcast.6), kind=kOutput, calls=%fused_computation | convolution fusion | flops 1343488000 | bytes 4980736 | tf_op jit(solution)/shard_map/dot_general | solution.py:402

commit v4 on v3

--- a/solution.py
+++ b/solution.py
@@ -11,9 +11,10 @@
 GROUPS = 8
 PLANE = 32
 UNITS = 4
+AHEAD = 2
 OFFSETS = (
-    (0, 0), (1, 0), (0, 1), (1, 1), (2, 0), (1, 3), (2, 2), (0, 2),
-    (2, 1), (2, 3), (1, 2), (3, 2), (3, 1), (3, 3), (3, 0), (0, 3),
+    (0, 0), (1, 0), (0, 1), (1, 1), (2, 0), (0, 2), (2, 1), (2, 3),
+    (1, 2), (3, 2), (2, 2), (3, 3), (1, 3), (3, 1), (3, 0), (0, 3),
 )
 PAIRS = 4
 IMG = 4
@@ -159,17 +160,21 @@
             .reshape(PLANE, 16, TILE)
         )
     pl.semaphore_wait(barrier, len(partners))
-    for g in range(GROUPS):
+
+    def send_plane(g):
         for u in range(UNITS):
             s = device_at(g, u, 1)
             land = xa.at[g, (u // 2) * 2 + core]
-            if g == 0 and u == 0:
+            if isinstance(g, int) and g == 0 and u == 0:
                 pltpu.make_async_copy(slots.at[s], land, xa_recv.at[g]).start()
             else:
                 pltpu.make_async_remote_copy(
-                    slots.at[s], land, xa_send.at[g], xa_recv.at[g],
+                    slots.at[s], land, xa_send, xa_recv.at[g],
                     device_id=at(s, z), device_id_type=MESH,
                 ).start()
+
+    for g in range(AHEAD):
+        send_plane(g)
 
     for b in range(IMG):
         scores = logits[b]
@@ -196,6 +201,7 @@
         ).start()
 
     def dispatch(g):
+        pl.when(g + AHEAD < GROUPS)(functools.partial(send_plane, g + AHEAD))
         arrived(xa.at[g], xa_recv.at[g])
         for n in range(D // TILE):
             cols = pl.ds(n * TILE, TILE)
@@ -206,12 +212,12 @@
                 .astype(BF16)
                 .reshape(PAIRS, 16, TILE)
             )
-        send(za.at[g, pair], rows.at[g, 4], z_send.at[g, 0], z_recv.at[g, 0], along_z(-1))
+        send(za.at[g, pair], rows.at[g, 4], z_send, f_recv.at[g], along_z(-1))
         for slot, step in ((3, 3), (2, -2), (1, 1)):
             zz = along_z(step)
             send(
                 za.at[g, lax.div(zz, 2)], rows.at[g, slot],
-                z_send.at[g, slot], z_recv.at[g, slot], zz,
+                z_send, z_recv.at[g, slot - 1], zz,
             )
         rows[g, 0] = za[g, pair]
 
@@ -240,16 +246,12 @@
 
     def forward(g):
         for j in (3, 2, 1):
-            arrived(rows.at[g, j], z_recv.at[g, j])
-            send(
-                rows.at[g, j], rows.at[g, 4 + j], f_send.at[g, j], f_recv.at[g, j], along_z(-1)
-            )
+            arrived(rows.at[g, j], z_recv.at[g, j - 1])
+            send(rows.at[g, j], rows.at[g, 4 + j], f_send, f_recv.at[g], along_z(-1))
 
     def experts(g):
         keep_flags(g)
-        arrived(rows.at[g, 4], z_recv.at[g, 0])
-        for j in (1, 2, 3):
-            arrived(rows.at[g, 4 + j], f_recv.at[g, j])
+        arrived(rows.at[g, pl.ds(4, 4)], f_recv.at[g])
 
         def first(n, carry):
             cols = pl.ds(pl.multiple_of(n * TILE, TILE), TILE)
@@ -266,27 +268,23 @@
 
         lax.fori_loop(0, D // TILE, first, 0)
         lax.fori_loop(0, D // TILE, second, 0)
-        for j in (3, 2, 1, 0):
-            send(
-                part.at[g, 4 + j], other.at[g, j], q_send.at[g, j], q_recv.at[g, j], along_z(-1)
-            )
+        for half in (1, 0):
+            src, dst = part.at[g, pl.ds(4 + 2 * half, 2)], other.at[g, pl.ds(2 * half, 2)]
+            send(src, dst, q_send, q_recv.at[g, half], along_z(-1))
 
     def gather_pair(g):
         for j in (3, 2, 1, 0):
-            arrived(other.at[g, j], q_recv.at[g, j])
+            if j % 2:
+                arrived(other.at[g, pl.ds(j - 1, 2)], q_recv.at[g, j // 2])
             value = (part[g, j].astype(F32) + other[g, j].astype(F32)).astype(BF16)
             if j == 0:
                 back[g, pair] = value
             else:
                 total[g, j] = value
-                send(
-                    total.at[g, j], back.at[g, pair],
-                    t_send.at[g, j], t_recv.at[g, j], along_z(j),
-                )
+                send(total.at[g, j], back.at[g, pair], t_send, t_recv.at[g], along_z(j))
 
     def give_back(g):
-        for slot, step in ((1, 1), (2, -2), (3, 3)):
-            arrived(back.at[g, lax.div(along_z(step), 2)], t_recv.at[g, slot])
+        arrived(back.at[g, pl.ds(0, 3)], t_recv.at[g])
         for n in range(D // TILE):
             cols = pl.ds(n * TILE, TILE)
             xb[g, :, :, cols] = (
@@ -300,11 +298,11 @@
         for u in range(UNITS):
             s = device_at(g, u, -1)
             gone = xb.at[g, (u // 2) * 2 + (core if u % 2 == 0 else 1 - core)]
-            land = xb_recv.at[g, u // 2]
+            land = xb_recv.at[g]
 
             def start_remote(s=s, gone=gone, land=land):
                 pltpu.make_async_remote_copy(
-                    gone, out_h.at[me], xb_send.at[g], land,
+                    gone, out_h.at[me], xb_send, land,
                     device_id=at(s, z), device_id_type=MESH,
                 ).start()
 
@@ -329,18 +327,15 @@
     lax.fori_loop(0, GROUPS + len(stages) - 1, turn, 0)
 
     spread_out.wait()
+    remote = slots.at[pl.ds(0, PLANE - 1)]
+    arrived(remote, xa_send)
+    arrived(za, z_send)
+    arrived(part.at[pl.ds(0, 3)], f_send)
+    arrived(other, q_send)
+    arrived(part.at[pl.ds(0, 3)], t_send)
+    arrived(remote, xb_send)
     for g in range(GROUPS):
-        remote = pl.ds(1, UNITS - 1) if g == 0 else pl.ds(0, UNITS)
-        arrived(xa.at[g, remote], xa_send.at[g])
-        for slot in range(4):
-            arrived(za.at[g, slot], z_send.at[g, slot])
-            arrived(part.at[g, 4 + slot], q_send.at[g, slot])
-            if slot:
-                arrived(rows.at[g, slot], f_send.at[g, slot])
-                arrived(total.at[g, slot], t_send.at[g, slot])
-        arrived(xb.at[g, remote], xb_send.at[g])
-        for chip in range(2):
-            arrived(out_h.at[pl.ds(chip_at(g, chip, 1) * 2, 2)], xb_recv.at[g, chip])
+        arrived(out_h.at[pl.ds(0, UNITS)], xb_recv.at[g])
 
 
 def exchange(images, router, w_in, w_out, words):
@@ -382,12 +377,12 @@
             pltpu.VMEM((128, D), BF16),
             pltpu.VMEM((IMG * PATCHES, IMG * E), BF16),
             dma((11,)),
-            dma((GROUPS,)), dma((GROUPS,)),
-            dma((GROUPS, 4)), dma((GROUPS, 4)),
-            dma((GROUPS, 4)), dma((GROUPS, 4)),
-            dma((GROUPS, 4)), dma((GROUPS, 4)),
-            dma((GROUPS, 4)), dma((GROUPS, 4)),
-            dma((GROUPS,)), dma((GROUPS, 2)),
+            dma, dma((GROUPS,)),
+            dma, dma((GROUPS, 3)),
+            dma, dma((GROUPS,)),
+            dma, dma((GROUPS, 2)),
+            dma, dma((GROUPS,)),
+            dma, dma((GROUPS,)),
             dma,
         ],
         compiler_params=pltpu.CompilerParams(

time: 123 us -> 119 us (0.967)
  Pallas kernels: 118 us -> 114 us
    pallas_call x1, Pallas kernels: 118 us -> 114 us  [exchange(): pl.pallas_call(kernel, out_shape=(jax.ShapeDtypeStruct((PLANE, 16, D), BF...]
where the time goes in v4:
time: 119 us
  Pallas kernels  114 us (96%)
  matrix products  4.65 us (4%)
    pallas_call x1, Pallas kernels, exchange(): pl.pallas_call(kernel, out_shape=(jax.ShapeDtypeStruct((PLANE, 16, D), BF...  114 us
    dot_general x1, matrix products, on_device(): mixed = jnp.dot(spread, arrived.reshape(512, D), preferred_element_type=F32)  4.65 us

profile of v4, /device:TPU:1, one launch (start us, length us, event | category | flops | bytes accessed | tf_op | source)
XLA Modules:
  0.0 118.6 jit_solution(1143937171025373623)
XLA Ops:
  0.0 114.0 %shard_map.82 = (bf16[32,16,1280]{2,1,0:T(8,128)(2,1)}, bf16[1024,512]{1,0:T(8,128)(2,1)}) custom-call(bf16[4,256,1280]{2,1,0:T(8,128)(2,1)} %img_h.1, bf16[1280,128]{1,0:T(8,128)(2,1)} %router_h.1, bf16[1,1280,1280]{2,1,0:T(8,128)(2,1)} %w1_h.1, bf16[1,1280,1280]{2,1,0:T(8,128)(2,1)} %w2_h.1, s32[1024,128]{1,0:T(8,128)} %bitcast.5, ...), custom_call_target="tpu_custom_call" | custom-call | tf_op jit(solution)/shard_map/pallas_call | solution.py:347
  114.0 4.7 %convolution_convert_fusion = bf16[1024,1280]{1,0:T(8,128)(2,1)} fusion(bf16[1024,512]{1,0:T(8,128)(2,1)} %get-tuple-element.7, bf16[512,1280]{1,0:T(8,128)(2,1)} %bitcast.6), kind=kOutput, calls=%fused_computation | convolution fusion | flops 1343488000 | bytes 4980736 | tf_op jit(solution)/shard_map/dot_general | solution.py:397

commit v5 on v4

--- a/solution.py
+++ b/solution.py
@@ -13,8 +13,8 @@
 UNITS = 4
 AHEAD = 2
 OFFSETS = (
-    (0, 0), (1, 0), (0, 1), (1, 1), (2, 0), (0, 2), (2, 1), (2, 3),
-    (1, 2), (3, 2), (2, 2), (3, 3), (1, 3), (3, 1), (3, 0), (0, 3),
+    (0, 0), (1, 0), (0, 1), (0, 3), (2, 0), (0, 2), (2, 1), (2, 3),
+    (1, 2), (3, 2), (2, 2), (3, 3), (1, 3), (3, 1), (3, 0), (1, 1),
 )
 PAIRS = 4
 IMG = 4
@@ -72,7 +72,7 @@
 def kernel(
     img_h, router_h, w1_h, w2_h, kb_h, order_h, pairs_h, bits_h,
     out_h, spread_h,
-    img, router, w1, w2, kb, order, pairs, bits, words, logits, raw, slots,
+    img, router, w1, w2, kb, order, pairs, bits, words, logits, raw, slots, first_slots,
     xa, za, rows, part, other, total, back, xb, hidden, keep, spread,
     load_sem, xa_send, xa_recv, z_send, z_recv, f_send, f_recv,
     q_send, q_recv, t_send, t_recv, xb_send, xb_recv, out_sem,
@@ -105,11 +105,9 @@
         return chip_at(g, unit // 2, sign) * 2 + side
 
     loads = [
-        (img_h.at[0], img.at[0]),
+        (img_h.at[pl.ds(0, 2)], img.at[pl.ds(0, 2)]),
         (router_h, router),
-        (img_h.at[1], img.at[1]),
-        (img_h.at[2], img.at[2]),
-        (img_h.at[3], img.at[3]),
+        (img_h.at[pl.ds(2, 2)], img.at[pl.ds(2, 2)]),
         (order_h, order),
         (pairs_h, pairs),
         (kb_h, kb),
@@ -120,7 +118,7 @@
     copies = [
         pltpu.make_async_copy(src, dst, load_sem.at[i]) for i, (src, dst) in enumerate(loads)
     ]
-    for copy in copies:
+    for copy in copies[:4]:
         copy.start()
 
     barrier = pltpu.get_barrier_semaphore()
@@ -134,24 +132,58 @@
     for partner in partners:
         pl.semaphore_signal(barrier, inc=1, device_id=partner, device_id_type=MESH)
 
-    for b in range(IMG):
-        if b == 0:
-            copies[0].wait()
-            copies[1].wait()
-        else:
-            copies[1 + b].wait()
-        scores = jnp.dot(img[b], router[...], preferred_element_type=F32)
-        logits[b] = scores
-        top = jnp.max(scores, axis=0, keepdims=True)
-        grown = jnp.exp(scores - top)
-        share = (grown / jnp.sum(grown, axis=0, keepdims=True)).astype(BF16)
-        for n in range(D // TILE):
-            cols = pl.ds(n * TILE, TILE)
-            raw[pl.ds(b * E, E), cols] = lax.dot_general(
-                share, img[b, :, cols], (((0,), (0,)), ((), ())), preferred_element_type=F32
-            ).astype(BF16)
-
-    copies[5].wait()
+    copies[1].wait()
+    for half in range(2):
+        copies[2 * half].wait()
+        both = jnp.dot(
+            img[pl.ds(2 * half, 2)].reshape(2 * PATCHES, D), router[...],
+            preferred_element_type=F32,
+        )
+        for b in (2 * half, 2 * half + 1):
+            scores = both[(b % 2) * PATCHES : (b % 2 + 1) * PATCHES]
+            logits[b] = scores
+            top = jnp.max(scores, axis=0, keepdims=True)
+            grown = jnp.exp(scores - top)
+            share = (grown / jnp.sum(grown, axis=0, keepdims=True)).astype(BF16)
+            for n in range(D // TILE):
+                cols = pl.ds(n * TILE, TILE)
+                raw[pl.ds(b * E, E), cols] = lax.dot_general(
+                    share, img[b, :, cols], (((0,), (0,)), ((), ())), preferred_element_type=F32
+                ).astype(BF16)
+
+    for copy in copies[4:]:
+        copy.start()
+    copies[3].wait()
+    near = jnp.concatenate(
+        [order[pl.ds(pl.multiple_of(chip_at(0, c, 1) * 32, 32), 32), :] for c in range(2)], axis=0
+    )
+    for n in range(D // TILE):
+        cols = pl.ds(n * TILE, TILE)
+        first_slots[:, :, cols] = (
+            jnp.dot(near, raw[:, cols], preferred_element_type=F32)
+            .astype(BF16)
+            .reshape(UNITS, 16, TILE)
+        )
+    pl.semaphore_wait(barrier, len(partners))
+
+    def send_plane(g):
+        for u in range(UNITS):
+            s = device_at(g, u, 1)
+            land = xa.at[g, (u // 2) * 2 + core]
+            early = isinstance(g, int) and g == 0
+            if early:
+                src = first_slots.at[(u // 2) * 2 + lax.rem(s, 2)]
+            else:
+                src = slots.at[s]
+            if early and u == 0:
+                pltpu.make_async_copy(src, land, xa_recv.at[g]).start()
+            else:
+                pltpu.make_async_remote_copy(
+                    src, land, xa_send, xa_recv.at[g],
+                    device_id=at(s, z), device_id_type=MESH,
+                ).start()
+
+    send_plane(0)
     for n in range(D // TILE):
         cols = pl.ds(n * TILE, TILE)
         slots[:, :, cols] = (
@@ -159,21 +191,7 @@
             .astype(BF16)
             .reshape(PLANE, 16, TILE)
         )
-    pl.semaphore_wait(barrier, len(partners))
-
-    def send_plane(g):
-        for u in range(UNITS):
-            s = device_at(g, u, 1)
-            land = xa.at[g, (u // 2) * 2 + core]
-            if isinstance(g, int) and g == 0 and u == 0:
-                pltpu.make_async_copy(slots.at[s], land, xa_recv.at[g]).start()
-            else:
-                pltpu.make_async_remote_copy(
-                    slots.at[s], land, xa_send, xa_recv.at[g],
-                    device_id=at(s, z), device_id_type=MESH,
-                ).start()
-
-    for g in range(AHEAD):
+    for g in range(1, AHEAD):
         send_plane(g)
 
     for b in range(IMG):
@@ -186,10 +204,10 @@
     spread_out = pltpu.make_async_copy(spread, spread_h, out_sem)
     spread_out.start()
 
-    copies[7].wait()
+    copies[5].wait()
     words[:, pl.ds(0, 128)] = jnp.right_shift(kb[...], 5).astype(F32).astype(BF16)
     words[:, pl.ds(128, 128)] = jnp.bitwise_and(kb[...], 31).astype(F32).astype(BF16)
-    for i in (6, 8, 9, 10):
+    for i in (4, 6, 7, 8):
         copies[i].wait()
 
     def arrived(ref, sem):
@@ -250,7 +268,6 @@
             send(rows.at[g, j], rows.at[g, 4 + j], f_send, f_recv.at[g], along_z(-1))
 
     def experts(g):
-        keep_flags(g)
         arrived(rows.at[g, pl.ds(4, 4)], f_recv.at[g])
 
         def first(n, carry):
@@ -268,20 +285,15 @@
 
         lax.fori_loop(0, D // TILE, first, 0)
         lax.fori_loop(0, D // TILE, second, 0)
-        for half in (1, 0):
-            src, dst = part.at[g, pl.ds(4 + 2 * half, 2)], other.at[g, pl.ds(2 * half, 2)]
-            send(src, dst, q_send, q_recv.at[g, half], along_z(-1))
+        send(part.at[g, pl.ds(4, 4)], other.at[g], q_send, q_recv.at[g], along_z(-1))
+        pl.when(g + 1 < GROUPS)(functools.partial(keep_flags, g + 1))
 
     def gather_pair(g):
-        for j in (3, 2, 1, 0):
-            if j % 2:
-                arrived(other.at[g, pl.ds(j - 1, 2)], q_recv.at[g, j // 2])
-            value = (part[g, j].astype(F32) + other[g, j].astype(F32)).astype(BF16)
-            if j == 0:
-                back[g, pair] = value
-            else:
-                total[g, j] = value
-                send(total.at[g, j], back.at[g, pair], t_send, t_recv.at[g], along_z(j))
+        arrived(other.at[g], q_recv.at[g])
+        for j in (3, 2, 1):
+            total[g, j] = (part[g, j].astype(F32) + other[g, j].astype(F32)).astype(BF16)
+            send(total.at[g, j], back.at[g, pair], t_send, t_recv.at[g], along_z(j))
+        back[g, pair] = (part[g, 0].astype(F32) + other[g, 0].astype(F32)).astype(BF16)
 
     def give_back(g):
         arrived(back.at[g, pl.ds(0, 3)], t_recv.at[g])
@@ -316,15 +328,23 @@
 
                 pl.when(g > 0)(start_remote)
 
-    stages = (dispatch, forward, experts, gather_pair, give_back)
+    stages = (
+        (0, dispatch),
+        (1, forward),
+        (3, experts),
+        (4, gather_pair),
+        (5, give_back),
+    )
+
+    keep_flags(0)
 
     def turn(t, carry):
-        for lag, stage in enumerate(stages):
+        for lag, stage in stages:
             g = t - lag
             pl.when(jnp.logical_and(g >= 0, g < GROUPS))(functools.partial(stage, g))
         return carry
 
-    lax.fori_loop(0, GROUPS + len(stages) - 1, turn, 0)
+    lax.fori_loop(0, GROUPS + max(lag for lag, _ in stages), turn, 0)
 
     spread_out.wait()
     remote = slots.at[pl.ds(0, PLANE - 1)]
@@ -365,6 +385,7 @@
             pltpu.VMEM((IMG, PATCHES, E), F32),
             pltpu.VMEM((IMG * E, D), BF16),
             pltpu.VMEM((PLANE, 16, D), BF16),
+            pltpu.VMEM((UNITS, 16, D), BF16),
             pltpu.VMEM((GROUPS, UNITS, 16, D), BF16),
             pltpu.VMEM((GROUPS, PAIRS, 16, D), BF16),
             pltpu.VMEM((GROUPS, 8, 16, D), BF16),
@@ -376,11 +397,11 @@
             pltpu.VMEM((128, D), BF16),
             pltpu.VMEM((128, D), BF16),
             pltpu.VMEM((IMG * PATCHES, IMG * E), BF16),
-            dma((11,)),
+            dma((9,)),
             dma, dma((GROUPS,)),
             dma, dma((GROUPS, 3)),
             dma, dma((GROUPS,)),
-            dma, dma((GROUPS, 2)),
+            dma, dma((GROUPS,)),
             dma, dma((GROUPS,)),
             dma, dma((GROUPS,)),
             dma,

time: 119 us -> 115 us (0.966)
  Pallas kernels: 114 us -> 110 us
    pallas_call x1, Pallas kernels: 114 us -> 110 us  [exchange(): pl.pallas_call(kernel, out_shape=(jax.ShapeDtypeStruct((PLANE, 16, D), BF...]
where the time goes in v5:
time: 115 us; the launch traced here: 114 us
  Pallas kernels  110 us (96%)
  matrix products  4.65 us (4%)
    pallas_call x1, Pallas kernels, exchange(): pl.pallas_call(kernel, out_shape=(jax.ShapeDtypeStruct((PLANE, 16, D), BF...  110 us
    dot_general x1, matrix products, on_device(): mixed = jnp.dot(spread, arrived.reshape(512, D), preferred_element_type=F32)  4.65 us

profile of v5, /device:TPU:1, one launch (start us, length us, event | category | flops | bytes accessed | tf_op | source)
XLA Modules:
  0.0 114.5 jit_solution(10872653559351492139)
XLA Ops:
  0.0 109.8 %shard_map.82 = (bf16[32,16,1280]{2,1,0:T(8,128)(2,1)}, bf16[1024,512]{1,0:T(8,128)(2,1)}) custom-call(bf16[4,256,1280]{2,1,0:T(8,128)(2,1)} %img_h.1, bf16[1280,128]{1,0:T(8,128)(2,1)} %router_h.1, bf16[1,1280,1280]{2,1,0:T(8,128)(2,1)} %w1_h.1, bf16[1,1280,1280]{2,1,0:T(8,128)(2,1)} %w2_h.1, s32[1024,128]{1,0:T(8,128)} %bitcast.5, ...), custom_call_target="tpu_custom_call" | custom-call | tf_op jit(solution)/shard_map/pallas_call | solution.py:367
  109.8 4.7 %convolution_convert_fusion = bf16[1024,1280]{1,0:T(8,128)(2,1)} fusion(bf16[1024,512]{1,0:T(8,128)(2,1)} %get-tuple-element.7, bf16[512,1280]{1,0:T(8,128)(2,1)} %bitcast.6), kind=kOutput, calls=%fused_computation | convolution fusion | flops 1343488000 | bytes 4980736 | tf_op jit(solution)/shard_map/dot_general | solution.py:418

commit v6 on v5

--- a/solution.py
+++ b/solution.py
@@ -118,7 +118,7 @@
     copies = [
         pltpu.make_async_copy(src, dst, load_sem.at[i]) for i, (src, dst) in enumerate(loads)
     ]
-    for copy in copies[:4]:
+    for copy in copies[:3]:
         copy.start()
 
     barrier = pltpu.get_barrier_semaphore()
@@ -135,6 +135,8 @@
     copies[1].wait()
     for half in range(2):
         copies[2 * half].wait()
+        if half == 0:
+            copies[3].start()
         both = jnp.dot(
             img[pl.ds(2 * half, 2)].reshape(2 * PATCHES, D), router[...],
             preferred_element_type=F32,
@@ -194,21 +196,7 @@
     for g in range(1, AHEAD):
         send_plane(g)
 
-    for b in range(IMG):
-        scores = logits[b]
-        grown = jnp.exp(scores - jnp.max(scores, axis=1, keepdims=True))
-        share = (grown / jnp.sum(grown, axis=1, keepdims=True)).astype(BF16)
-        spread[pl.ds(b * PATCHES, PATCHES), :] = lax.dot_general(
-            share, order[:, pl.ds(b * E, E)], (((1,), (1,)), ((), ())), preferred_element_type=F32
-        ).astype(BF16)
-    spread_out = pltpu.make_async_copy(spread, spread_h, out_sem)
-    spread_out.start()
-
-    copies[5].wait()
-    words[:, pl.ds(0, 128)] = jnp.right_shift(kb[...], 5).astype(F32).astype(BF16)
-    words[:, pl.ds(128, 128)] = jnp.bitwise_and(kb[...], 31).astype(F32).astype(BF16)
-    for i in (4, 6, 7, 8):
-        copies[i].wait()
+    copies[4].wait()
 
     def arrived(ref, sem):
         pltpu.make_async_copy(ref, ref, sem).wait()
@@ -219,7 +207,6 @@
         ).start()
 
     def dispatch(g):
-        pl.when(g + AHEAD < GROUPS)(functools.partial(send_plane, g + AHEAD))
         arrived(xa.at[g], xa_recv.at[g])
         for n in range(D // TILE):
             cols = pl.ds(n * TILE, TILE)
@@ -237,6 +224,7 @@
                 za.at[g, lax.div(zz, 2)], rows.at[g, slot],
                 z_send, z_recv.at[g, slot - 1], zz,
             )
+        pl.when(g + AHEAD < GROUPS)(functools.partial(send_plane, g + AHEAD))
         rows[g, 0] = za[g, pair]
 
     def keep_flags(g):
@@ -283,8 +271,8 @@
             part[g, :, :, cols] = value.astype(BF16).reshape(8, 16, TILE)
             return carry
 
-        lax.fori_loop(0, D // TILE, first, 0)
-        lax.fori_loop(0, D // TILE, second, 0)
+        lax.fori_loop(0, D // TILE, first, 0, unroll=True)
+        lax.fori_loop(0, D // TILE, second, 0, unroll=True)
         send(part.at[g, pl.ds(4, 4)], other.at[g], q_send, q_recv.at[g], along_z(-1))
         pl.when(g + 1 < GROUPS)(functools.partial(keep_flags, g + 1))
 
@@ -336,17 +324,33 @@
         (5, give_back),
     )
 
-    keep_flags(0)
+    def prepare():
+        for b in range(IMG):
+            scores = logits[b]
+            grown = jnp.exp(scores - jnp.max(scores, axis=1, keepdims=True))
+            share = (grown / jnp.sum(grown, axis=1, keepdims=True)).astype(BF16)
+            spread[pl.ds(b * PATCHES, PATCHES), :] = lax.dot_general(
+                share, order[:, pl.ds(b * E, E)], (((1,), (1,)), ((), ())), preferred_element_type=F32
+            ).astype(BF16)
+        pltpu.make_async_copy(spread, spread_h, out_sem).start()
+
+        copies[5].wait()
+        words[:, pl.ds(0, 128)] = jnp.right_shift(kb[...], 5).astype(F32).astype(BF16)
+        words[:, pl.ds(128, 128)] = jnp.bitwise_and(kb[...], 31).astype(F32).astype(BF16)
+        for i in (6, 7, 8):
+            copies[i].wait()
+        keep_flags(0)
 
     def turn(t, carry):
         for lag, stage in stages:
             g = t - lag
             pl.when(jnp.logical_and(g >= 0, g < GROUPS))(functools.partial(stage, g))
+        pl.when(t == 0)(prepare)
         return carry
 
     lax.fori_loop(0, GROUPS + max(lag for lag, _ in stages), turn, 0)
 
-    spread_out.wait()
+    pltpu.make_async_copy(spread, spread_h, out_sem).wait()
     remote = slots.at[pl.ds(0, PLANE - 1)]
     arrived(remote, xa_send)
     arrived(za, z_send)

time: 115 us -> 114 us (level)
  no operation moved by 1% of the time
where the time goes in v6:
time: 114 us
  Pallas kernels  110 us (96%)
  matrix products  4.66 us (4%)
    pallas_call x1, Pallas kernels, exchange(): pl.pallas_call(kernel, out_shape=(jax.ShapeDtypeStruct((PLANE, 16, D), BF...  110 us
    dot_general x1, matrix products, on_device(): mixed = jnp.dot(spread, arrived.reshape(512, D), preferred_element_type=F32)  4.66 us

profile of v6, /device:TPU:1, one launch (start us, length us, event | category | flops | bytes accessed | tf_op | source)
XLA Modules:
  0.0 114.2 jit_solution(16101503657537284785)
XLA Ops:
  0.0 109.5 %shard_map.82 = (bf16[32,16,1280]{2,1,0:T(8,128)(2,1)}, bf16[1024,512]{1,0:T(8,128)(2,1)}) custom-call(bf16[4,256,1280]{2,1,0:T(8,128)(2,1)} %img_h.1, bf16[1280,128]{1,0:T(8,128)(2,1)} %router_h.1, bf16[1,1280,1280]{2,1,0:T(8,128)(2,1)} %w1_h.1, bf16[1,1280,1280]{2,1,0:T(8,128)(2,1)} %w2_h.1, s32[1024,128]{1,0:T(8,128)} %bitcast.5, ...), custom_call_target="tpu_custom_call" | custom-call | tf_op jit(solution)/shard_map/pallas_call | solution.py:371
  109.5 4.7 %convolution_convert_fusion = bf16[1024,1280]{1,0:T(8,128)(2,1)} fusion(bf16[1024,512]{1,0:T(8,128)(2,1)} %get-tuple-element.7, bf16[512,1280]{1,0:T(8,128)(2,1)} %bitcast.6), kind=kOutput, calls=%fused_computation | convolution fusion | flops 1343488000 | bytes 4980736 | tf_op jit(solution)/shard_map/dot_general | solution.py:422

commit v7 on v6

--- a/solution.py
+++ b/solution.py
@@ -248,7 +248,7 @@
             keep[:, cols] = flag.astype(F32).astype(BF16)
             return carry
 
-        lax.fori_loop(0, D // TILE, tile, 0)
+        lax.fori_loop(0, D // TILE, tile, 0, unroll=True)
 
     def forward(g):
         for j in (3, 2, 1):

time: 114 us -> 114 us (level)
  no operation moved by 1% of the time
where the time goes in v7:
time: 114 us
  Pallas kernels  110 us (96%)
  matrix products  4.66 us (4%)
    pallas_call x1, Pallas kernels, exchange(): pl.pallas_call(kernel, out_shape=(jax.ShapeDtypeStruct((PLANE, 16, D), BF...  110 us
    dot_general x1, matrix products, on_device(): mixed = jnp.dot(spread, arrived.reshape(512, D), preferred_element_type=F32)  4.66 us

profile of v7, /device:TPU:1, one launch (start us, length us, event | category | flops | bytes accessed | tf_op | source)
XLA Modules:
  0.0 114.2 jit_solution(9879966776889567774)
XLA Ops:
  0.0 109.5 %shard_map.82 = (bf16[32,16,1280]{2,1,0:T(8,128)(2,1)}, bf16[1024,512]{1,0:T(8,128)(2,1)}) custom-call(bf16[4,256,1280]{2,1,0:T(8,128)(2,1)} %img_h.1, bf16[1280,128]{1,0:T(8,128)(2,1)} %router_h.1, bf16[1,1280,1280]{2,1,0:T(8,128)(2,1)} %w1_h.1, bf16[1,1280,1280]{2,1,0:T(8,128)(2,1)} %w2_h.1, s32[1024,128]{1,0:T(8,128)} %bitcast.5, ...), custom_call_target="tpu_custom_call" | custom-call | tf_op jit(solution)/shard_map/pallas_call | solution.py:371
  109.5 4.7 %convolution_convert_fusion = bf16[1024,1280]{1,0:T(8,128)(2,1)} fusion(bf16[1024,512]{1,0:T(8,128)(2,1)} %get-tuple-element.7, bf16[512,1280]{1,0:T(8,128)(2,1)} %bitcast.6), kind=kOutput, calls=%fused_computation | convolution fusion | flops 1343488000 | bytes 4980736 | tf_op jit(solution)/shard_map/dot_general | solution.py:422
